TPU v7x, 512 devices: a whole 4x4x16 slice. The times are simulated.
512 devices in a mesh: pipe: 8 (over x_hi, y), expert: 64 (over z, x_lo, core).
Axes of the slice: x: 4 (x_hi: 2, x_lo: 2; x = x_hi * 2 + x_lo), y: 4, z: 16, core: 2. Of those that a mesh axis runs over, the one named last changes fastest.
Arguments:
- activations: bfloat16 [8, 768, 3584], P('pipe', 'expert'), may hold values from -6 to 6
- out_grads: bfloat16 [8, 768, 3584], P('pipe', 'expert'), may hold values from -6 to 6
- gate_vals: float32 [8, 768, 8], P('pipe', 'expert'), may hold values from 0.05 to 0.3
- routes: int32 [8, 768, 8], P('pipe', 'expert'), may hold values from 0 to 15, all different within a row; in each aligned block of 12 rows (0 to 11, 12 to 23, ..., all dimensions but the last counted through in order) at most 9 rows name the same one
- up_weight: bfloat16 [8, 3584, 16384], P('pipe', None, 'expert'), may hold values from -0.09375 to 0.09375
- down_weight: bfloat16 [8, 16384, 3584], P('pipe', 'expert'), may hold values from -0.1875 to 0.1875
Outputs:
- handed_grads: bfloat16 [8, 768, 3584], P('pipe', 'expert')
- gate_grads: float32 [8, 768, 8], P('pipe', 'expert')
Inputs may be any that keep to these rules, and one draw needn't show every extreme that they name: `routes`: each token names 8 different experts; among the 12 tokens of one device at most 9 name the same expert, and on some device some expert is named by exactly 9 of them.
All inputs are finite; a program needn't handle non-finite values.
Results may differ from a plain program's by a relative error of at most 0.008.
Values may be sent and summed in bfloat16 or wider, within the bound.
No kernel may reach another device: no remote copies, remote signals or barrier semaphores. Data moves between devices by JAX's collectives and lax.ppermute only.
A program may use at most 128 MiB of HBM per device.

v0:
```python
import jax
import jax.numpy as jnp
from jax import lax
from jax.sharding import Mesh
from jax.sharding import PartitionSpec as P


EXPERTS = 16
LANES = 128


def swap(block, axis):
    return lax.ppermute(block, axis, [(0, 1), (1, 0)])


def along(block, step, cores=(0, 1)):
    depth = lax.axis_size("z")
    route = []
    for z in range(depth):
        for core in cores:
            to = (z + (step if core == 0 else -step)) % depth
            route.append((2 * z + core, 2 * to + core))
    return lax.ppermute(block, ("z", "c"), route)


def pieces(values):
    high = lax.reduce_precision(values, 8, 7)
    rest = values - high
    middle = lax.reduce_precision(rest, 8, 7)
    return high, middle, rest - middle


def after(value, *others):
    return lax.optimization_barrier((value, *others))[0]


def section(activations, out_grads, gate_vals, routes, up_weight, down_weight):
    inputs, upstream = activations[0], out_grads[0]
    gates, chosen = gate_vals[0], routes[0]
    local_up, local_down = up_weight[0], down_weight[0]
    tok, width = inputs.shape
    first = lax.axis_index("c") == 0
    expert = lax.axis_index("z")
    reach = lax.axis_size("z") // 2
    lane = jnp.arange(LANES)

    onehot = (chosen[:, :, None] == jnp.arange(EXPERTS, dtype=jnp.int32)).astype(jnp.float32)
    dense = jnp.sum(onehot * gates[:, :, None], axis=1)
    tail = jnp.concatenate(pieces(dense), axis=1).astype(jnp.bfloat16)
    tail = jnp.pad(tail, ((0, 0), (0, LANES - tail.shape[1])))
    tailed = jnp.concatenate([inputs, tail], axis=1)
    middle = width // 2

    def beside(rows):
        got = swap(rows, "c")
        return jnp.concatenate([jnp.where(first, rows, got), jnp.where(first, got, rows)], axis=0)

    blocks = [beside(tailed), beside(upstream)]

    halves = lambda whole: (whole[:middle], whole[middle:])
    far_up, passed_up = [None, None], [None, None]
    far_down = swap(local_down, "xl")

    current, kept = list(blocks), [[], []]
    for step in range(1, reach + 1):
        cores = (0, 1) if step < reach else (0,)
        for side in range(2):
            current[side] = along(current[side], 1, cores)
        lead = kept[0][-1] if step > 1 else blocks[0]
        if step == 2:
            far_up[0] = swap(after(local_up, lead)[:middle], "xl")
        if step == 3:
            far_up[1] = swap(after(local_up, lead)[middle:], "xl")
        if step == 4:
            near_down = swap(after(local_down, lead), "c")
        if step == 5:
            near_up = swap(after(local_up, lead), "c")
        if step == 7:
            passed_down = swap(after(far_down, lead), "c")
        if step == reach:
            passed_up[0] = swap(after(far_up[0], lead), "c")
            passed_up[1] = swap(after(far_up[1], current[0], passed_down), "c")
            current = [jnp.where(first, chain, own) for chain, own in zip(current, blocks)]
        for side, chain in zip(kept, current):
            side.append(chain)
    in_rows = jnp.concatenate(kept[0], axis=0)
    up_rows = jnp.concatenate(kept[1], axis=0)

    def dot(left, right, left_dim, right_dim):
        return lax.dot_general(
            left,
            right,
            (((left_dim,), (right_dim,)), ((), ())),
            preferred_element_type=jnp.float32,
        )

    def terms(down_part, low_part, high_part):
        hid_grad = dot(up_rows, down_part, 1, 1)
        pre_act = dot(in_rows[:, :middle], low_part, 1, 0)
        pre_act = pre_act + dot(in_rows[:, middle:width], high_part, 1, 0)
        sig_val = jax.nn.sigmoid(pre_act)
        act_grad = (hid_grad * (sig_val * (1.0 + pre_act * (1.0 - sig_val)))).astype(jnp.bfloat16)
        partial_dg = jnp.sum(hid_grad * (pre_act * sig_val), axis=1, keepdims=True)
        return dot(act_grad, low_part, 1, 1), dot(act_grad, high_part, 1, 1), partial_dg

    found = [terms(local_down, *halves(local_up)), terms(near_down, *halves(near_up))]
    done = (*found[0], *found[1])
    found.append(terms(after(far_down, *done), *[after(part, *done) for part in far_up]))
    found.append(terms(*[after(part, found[2][2]) for part in (passed_down, *passed_up)]))
    low_dx, high_dx, token_terms = (sum(column) for column in zip(*found))

    named = ((lane % EXPERTS == expert) & (lane < 3 * EXPERTS)).astype(jnp.float32)
    weight = jnp.sum(in_rows[:, width:].astype(jnp.float32) * named, axis=1, keepdims=True)
    spread = sum(
        piece * (lane == expert + at * EXPERTS).astype(jnp.float32)
        for at, piece in enumerate(pieces(token_terms))
    )
    packed = jnp.concatenate([low_dx * weight, high_dx * weight, spread], axis=1)
    parts = packed.astype(jnp.bfloat16).reshape(reach, 2 * tok, width + LANES)

    def plus(moved, more):
        return moved.astype(jnp.float32) + more.astype(jnp.float32)

    even, odd = parts[reach - 1], parts[reach - 2]
    for at in range(reach - 3, 0, -2):
        cores = (0, 1) if at < reach - 3 else (0,)
        even = plus(along(even, -2, cores), parts[at]).astype(jnp.bfloat16)
        odd = plus(along(odd, -2), after(parts[at - 1], even)).astype(jnp.bfloat16)
    own = jnp.where(first, 0.0, parts[reach - 1].astype(jnp.float32))
    carry = plus(along(even, -2), along(odd, -1)) + own
    keep = jnp.where(first, carry[:tok], carry[tok:])
    give = jnp.where(first, carry[tok:], carry[:tok])
    summed = keep + swap(give, "c")
    grad_bf = summed[:, :width].astype(jnp.bfloat16)
    token_dg = sum(summed[:, width + at : width + at + EXPERTS] for at in (0, EXPERTS, 2 * EXPERTS))
    gate_grad = jnp.sum(onehot * token_dg[:, None, :], axis=2)
    sections = lax.axis_size("pipe")
    handed = lax.ppermute(grad_bf[None], "pipe", [(i, i - 1) for i in range(1, sections)])
    return handed, gate_grad[None]


def solution(mesh):
    pipe, _ = mesh.axis_names
    sections, devices = mesh.devices.shape
    fine = Mesh(mesh.devices.reshape(sections, devices // 4, 2, 2), (pipe, "z", "xl", "c"))
    inner = ("z", "xl", "c")
    rows = P("pipe", inner, None)
    return jax.shard_map(
        section,
        mesh=fine,
        in_specs=(rows, rows, rows, rows, P("pipe", None, inner), rows),
        out_specs=(rows, rows),
        check_vma=False,
    )
```

profile of v0, /device:TPU:24, one launch (start us, length us, event | category | flops | bytes accessed | tf_op | source)
XLA Modules:
  0.0 216.9 jit_solution(15694732735656600507)
XLA Ops:
  3.4 1.9 collective-permute-start.9
  5.4 2.4 %collective-permute-start = (bf16[12,3584]{1,0:T(8,128)(2,1)}, bf16[12,3584]{1,0:T(8,128)(2,1)S(1)}, u32[]{:S(2)}, u32[]{:S(2)}) collective-permute-start(bf16[12,3584]{1,0:T(8,128)(2,1)} %bitcast.56), channel_id=1, source_target_pairs={{0,1},{1,0},{2,3},{3,2},{4,5},{5,4},{6,7},{7,6},{8,9},{9,8},{10,11... | collective-permute-start | bytes 258056 | tf_op jit(solution)/shard_map/ppermute | solution.py:13
  7.8 3.4 %collective-permute-start.20 = (bf16[256,3584]{1,0:T(8,128)(2,1)}, bf16[256,3584]{1,0:T(8,128)(2,1)}, u32[]{:S(2)}, u32[]{:S(2)}) collective-permute-start(bf16[256,3584]{1,0:T(8,128)(2,1)} %bitcast.60), channel_id=1, source_target_pairs={{0,2},{2,0},{1,3},{3,1},{4,6},{6,4},{5,7},{7,5},{8,10},{10,8},{9,1... | collective-permute-start | bytes 5505032 | tf_op jit(solution)/shard_map/ppermute | solution.py:13
  12.2 3.8 %collective-permute-start.1 = (bf16[24,3584]{1,0:T(8,128)(2,1)S(1)}, bf16[24,3584]{1,0:T(8,128)(2,1)S(1)}, u32[]{:S(2)}, u32[]{:S(2)}) collective-permute-start(bf16[24,3584]{1,0:T(8,128)(2,1)S(1)} %pad_maximum_fusion.2), channel_id=1, source_target_pairs={{0,4},{1,61},{4,8},{5,1},{8,12},{9,5},{12,16},{13,9},{16,20},{17,1... | collective-permute-start | bytes 516104 | tf_op jit(solution)/shard_map/ppermute | solution.py:23
  17.1 3.8 %collective-permute-start.10 = (bf16[24,3712]{1,0:T(8,128)(2,1)S(1)}, bf16[24,3712]{1,0:T(8,128)(2,1)S(1)}, u32[]{:S(2)}, u32[]{:S(2)}) collective-permute-start(bf16[24,3712]{1,0:T(8,128)(2,1)S(1)} %pad_maximum_fusion.1), channel_id=1, source_target_pairs={{0,4},{1,61},{4,8},{5,1},{8,12},{9,5},{12,16},{13,9},{16,20},{17,1... | collective-permute-start | bytes 534536 | tf_op jit(solution)/shard_map/ppermute | solution.py:23
  20.9 6.1 %collective-permute-done.1 = bf16[24,3584]{1,0:T(8,128)(2,1)S(1)} collective-permute-done((bf16[24,3584]{1,0:T(8,128)(2,1)S(1)}, bf16[24,3584]{1,0:T(8,128)(2,1)S(1)}, u32[]{:S(2)}, u32[]{:S(2)}) %collective-permute-start.1) | collective-permute-done | bytes 172064 | tf_op jit(solution)/shard_map/ppermute | solution.py:23
  27.0 1.9 collective-permute-start.2
  30.1 2.4 %collective-permute-start.21 = (bf16[1792,256]{1,0:T(8,128)(2,1)S(1)}, bf16[1792,256]{1,0:T(8,128)(2,1)S(1)}, u32[]{:S(2)}, u32[]{:S(2)}) collective-permute-start(bf16[1792,256]{1,0:T(8,128)(2,1)S(1)} %slice.101), channel_id=1, source_target_pairs={{0,2},{2,0},{1,3},{3,1},{4,6},{6,4},{5,7},{7,5},{8,10},{10,8},{9,1... | collective-permute-start | bytes 2752520 | tf_op jit(solution)/shard_map/ppermute | solution.py:13
  32.5 1.9 collective-permute-start.11
  37.4 3.7 %collective-permute-done.11 = bf16[24,3712]{1,0:T(8,128)(2,1)S(1)} collective-permute-done((bf16[24,3712]{1,0:T(8,128)(2,1)S(1)}, bf16[24,3712]{1,0:T(8,128)(2,1)S(1)}, u32[]{:S(2)}, u32[]{:S(2)}) %collective-permute-start.11) | collective-permute-done | bytes 178208 | tf_op jit(solution)/shard_map/ppermute | solution.py:23
  41.2 3.4 %collective-permute-start.22 = (bf16[1792,256]{1,0:T(8,128)(2,1)S(1)}, bf16[1792,256]{1,0:T(8,128)(2,1)S(1)}, u32[]{:S(2)}, u32[]{:S(2)}) collective-permute-start(bf16[1792,256]{1,0:T(8,128)(2,1)S(1)} %slice.102), channel_id=1, source_target_pairs={{0,2},{2,0},{1,3},{3,1},{4,6},{6,4},{5,7},{7,5},{8,10},{10,8},{9,1... | collective-permute-start | bytes 2752520 | tf_op jit(solution)/shard_map/ppermute | solution.py:13
  44.6 1.9 collective-permute-start.12
  46.6 1.9 collective-permute-start.4
  48.5 4.7 %collective-permute-done.12 = bf16[24,3712]{1,0:T(8,128)(2,1)S(1)} collective-permute-done((bf16[24,3712]{1,0:T(8,128)(2,1)S(1)}, bf16[24,3712]{1,0:T(8,128)(2,1)S(1)}, u32[]{:S(2)}, u32[]{:S(2)}) %collective-permute-start.12) | collective-permute-done | bytes 178208 | tf_op jit(solution)/shard_map/ppermute | solution.py:23
  53.2 1.9 collective-permute-start.18
  55.1 1.9 collective-permute-start.13
  57.1 6.6 %collective-permute-done.13 = bf16[24,3712]{1,0:T(8,128)(2,1)S(1)} collective-permute-done((bf16[24,3712]{1,0:T(8,128)(2,1)S(1)}, bf16[24,3712]{1,0:T(8,128)(2,1)S(1)}, u32[]{:S(2)}, u32[]{:S(2)}) %collective-permute-start.13) | collective-permute-done | bytes 178208 | tf_op jit(solution)/shard_map/ppermute | solution.py:23
  63.7 1.9 collective-permute-start.5
  65.6 6.6 %collective-permute-done.5 = bf16[24,3584]{1,0:T(8,128)(2,1)S(1)} collective-permute-done((bf16[24,3584]{1,0:T(8,128)(2,1)S(1)}, bf16[24,3584]{1,0:T(8,128)(2,1)S(1)}, u32[]{:S(2)}, u32[]{:S(2)}) %collective-permute-start.5) | collective-permute-done | bytes 172064 | tf_op jit(solution)/shard_map/ppermute | solution.py:23
  72.2 1.9 collective-permute-start.14
  74.1 6.6 %collective-permute-done.14 = bf16[24,3712]{1,0:T(8,128)(2,1)S(1)} collective-permute-done((bf16[24,3712]{1,0:T(8,128)(2,1)S(1)}, bf16[24,3712]{1,0:T(8,128)(2,1)S(1)}, u32[]{:S(2)}, u32[]{:S(2)}) %collective-permute-start.14) | collective-permute-done | bytes 178208 | tf_op jit(solution)/shard_map/ppermute | solution.py:23
  82.7 6.6 %collective-permute-done.6 = bf16[24,3584]{1,0:T(8,128)(2,1)S(1)} collective-permute-done((bf16[24,3584]{1,0:T(8,128)(2,1)S(1)}, bf16[24,3584]{1,0:T(8,128)(2,1)S(1)}, u32[]{:S(2)}, u32[]{:S(2)}) %collective-permute-start.6) | collective-permute-done | bytes 172064 | tf_op jit(solution)/shard_map/ppermute | solution.py:23
  91.2 6.6 %collective-permute-done.15 = bf16[24,3712]{1,0:T(8,128)(2,1)S(1)} collective-permute-done((bf16[24,3712]{1,0:T(8,128)(2,1)S(1)}, bf16[24,3712]{1,0:T(8,128)(2,1)S(1)}, u32[]{:S(2)}, u32[]{:S(2)}) %collective-permute-start.15) | collective-permute-done | bytes 178208 | tf_op jit(solution)/shard_map/ppermute | solution.py:23
  97.8 1.9 collective-permute-start.7
  99.8 6.6 %collective-permute-done.7 = bf16[24,3584]{1,0:T(8,128)(2,1)S(1)} collective-permute-done((bf16[24,3584]{1,0:T(8,128)(2,1)S(1)}, bf16[24,3584]{1,0:T(8,128)(2,1)S(1)}, u32[]{:S(2)}, u32[]{:S(2)}) %collective-permute-start.7) | collective-permute-done | bytes 172064 | tf_op jit(solution)/shard_map/ppermute | solution.py:23
  106.3 1.9 collective-permute-start.16
  108.3 6.6 %collective-permute-done.16 = bf16[24,3712]{1,0:T(8,128)(2,1)S(1)} collective-permute-done((bf16[24,3712]{1,0:T(8,128)(2,1)S(1)}, bf16[24,3712]{1,0:T(8,128)(2,1)S(1)}, u32[]{:S(2)}, u32[]{:S(2)}) %collective-permute-start.16) | collective-permute-done | bytes 178208 | tf_op jit(solution)/shard_map/ppermute | solution.py:23
  116.9 1.9 collective-permute-start.19
  118.8 4.6 %collective-permute-done.8 = bf16[24,3584]{1,0:T(8,128)(2,1)S(1)} collective-permute-done((bf16[24,3584]{1,0:T(8,128)(2,1)S(1)}, bf16[24,3584]{1,0:T(8,128)(2,1)S(1)}, u32[]{:S(2)}, u32[]{:S(2)}) %collective-permute-start.8) | collective-permute-done | bytes 172064 | tf_op jit(solution)/shard_map/ppermute | solution.py:23
  125.4 6.6 %collective-permute-done.17 = bf16[24,3712]{1,0:T(8,128)(2,1)S(1)} collective-permute-done((bf16[24,3712]{1,0:T(8,128)(2,1)S(1)}, bf16[24,3712]{1,0:T(8,128)(2,1)S(1)}, u32[]{:S(2)}, u32[]{:S(2)}) %collective-permute-start.17) | collective-permute-done | bytes 178208 | tf_op jit(solution)/shard_map/ppermute | solution.py:23
  134.7 2.4 %collective-permute-start.23 = (bf16[256,3584]{1,0:T(8,128)(2,1)}, bf16[256,3584]{1,0:T(8,128)(2,1)S(1)}, u32[]{:S(2)}, u32[]{:S(2)}) collective-permute-start(bf16[256,3584]{1,0:T(8,128)(2,1)} %collective-permute-done.20), channel_id=1, source_target_pairs={{0,1},{1,0},{2,3},{3,2},{4,5},{5,4},{6,7},{7,6},{8,9},{9,8},{10,11... | collective-permute-start | bytes 5505032 | tf_op jit(solution)/shard_map/ppermute | solution.py:13
  141.2 1.9 collective-permute-start.25
  144.3 2.3 %multiply_convert_fusion.1 = (bf16[192,256]{1,0:T(8,128)(2,1)S(1)}, f32[192]{0:T(256)S(1)}) fusion(f32[192,256]{1,0:T(8,128)S(1)} %convolution_add_fusion.3, bf16[192,3584]{1,0:T(8,128)(2,1)S(1)} %select_dynamic-update-slice_fusion.1, bf16[256,3584]{1,0:T(8,128)(2,1)} %collective-permute-done.20), kind=kOutput, calls=%fused_computation.55 | convolution fusion | flops 352911168 | bytes 3506944 | tf_op jit(solution)/shard_map/dot_general | solution.py:90
  150.5 2.2 collective-permute-start.26
  152.7 7.8 %collective-permute-start.30 = (bf16[24,3712]{1,0:T(8,128)(2,1)S(1)}, bf16[24,3712]{1,0:T(8,128)(2,1)S(1)}, u32[]{:S(2)}, u32[]{:S(2)}) collective-permute-start(bf16[24,3712]{1,0:T(8,128)(2,1)S(1)} %get-tuple-element.36), channel_id=1, source_target_pairs={{0,56},{1,9},{4,60},{5,13},{8,0},{9,17},{12,4},{13,21},{16,8},{17,... | collective-permute-start | bytes 534536 | tf_op jit(solution)/shard_map/ppermute | solution.py:23
  160.6 3.7 %collective-permute-start.27 = (bf16[24,3712]{1,0:T(8,128)(2,1)S(1)}, bf16[24,3712]{1,0:T(8,128)(2,1)S(1)}, u32[]{:S(2)}, u32[]{:S(2)}) collective-permute-start(bf16[24,3712]{1,0:T(8,128)(2,1)S(1)} %add_convert_fusion.5), channel_id=1, source_target_pairs={{0,56},{1,9},{4,60},{5,13},{8,0},{9,17},{12,4},{13,21},{16,8},{17,... | collective-permute-start | bytes 534536 | tf_op jit(solution)/shard_map/ppermute | solution.py:23
  164.3 2.5 %collective-permute-done.30 = bf16[24,3712]{1,0:T(8,128)(2,1)S(1)} collective-permute-done((bf16[24,3712]{1,0:T(8,128)(2,1)S(1)}, bf16[24,3712]{1,0:T(8,128)(2,1)S(1)}, u32[]{:S(2)}, u32[]{:S(2)}) %collective-permute-start.30) | collective-permute-done | bytes 178208 | tf_op jit(solution)/shard_map/ppermute | solution.py:23
  166.8 6.6 %collective-permute-start.31 = (bf16[24,3712]{1,0:T(8,128)(2,1)S(1)}, bf16[24,3712]{1,0:T(8,128)(2,1)S(1)}, u32[]{:S(2)}, u32[]{:S(2)}) collective-permute-start(bf16[24,3712]{1,0:T(8,128)(2,1)S(1)} %add_convert_fusion.2), channel_id=1, source_target_pairs={{0,56},{1,9},{4,60},{5,13},{8,0},{9,17},{12,4},{13,21},{16,8},{17,... | collective-permute-start | bytes 534536 | tf_op jit(solution)/shard_map/ppermute | solution.py:23
  173.4 1.9 collective-permute-start.28
  175.4 3.2 %collective-permute-done.31 = bf16[24,3712]{1,0:T(8,128)(2,1)S(1)} collective-permute-done((bf16[24,3712]{1,0:T(8,128)(2,1)S(1)}, bf16[24,3712]{1,0:T(8,128)(2,1)S(1)}, u32[]{:S(2)}, u32[]{:S(2)}) %collective-permute-start.31) | collective-permute-done | bytes 178208 | tf_op jit(solution)/shard_map/ppermute | solution.py:23
  178.7 6.5 %collective-permute-start.32 = (bf16[24,3712]{1,0:T(8,128)(2,1)S(1)}, bf16[24,3712]{1,0:T(8,128)(2,1)S(1)}, u32[]{:S(2)}, u32[]{:S(2)}) collective-permute-start(bf16[24,3712]{1,0:T(8,128)(2,1)S(1)} %add_convert_fusion.1), channel_id=1, source_target_pairs={{0,56},{1,9},{4,60},{5,13},{8,0},{9,17},{12,4},{13,21},{16,8},{17,... | collective-permute-start | bytes 534536 | tf_op jit(solution)/shard_map/ppermute | solution.py:23
  185.2 3.1 %collective-permute-done.32 = bf16[24,3712]{1,0:T(8,128)(2,1)S(1)} collective-permute-done((bf16[24,3712]{1,0:T(8,128)(2,1)S(1)}, bf16[24,3712]{1,0:T(8,128)(2,1)S(1)}, u32[]{:S(2)}, u32[]{:S(2)}) %collective-permute-start.32) | collective-permute-done | bytes 178208 | tf_op jit(solution)/shard_map/ppermute | solution.py:23
  188.3 3.7 %collective-permute-start.33 = (bf16[24,3712]{1,0:T(8,128)(2,1)S(1)}, bf16[24,3712]{1,0:T(8,128)(2,1)S(1)}, u32[]{:S(2)}, u32[]{:S(2)}) collective-permute-start(bf16[24,3712]{1,0:T(8,128)(2,1)S(1)} %add_convert_fusion), channel_id=1, source_target_pairs={{0,60},{1,5},{4,0},{5,9},{8,4},{9,13},{12,8},{13,17},{16,12},{17,2... | collective-permute-start | bytes 534536 | tf_op jit(solution)/shard_map/ppermute | solution.py:23
  192.0 4.7 %collective-permute-start.29 = (bf16[24,3712]{1,0:T(8,128)(2,1)S(1)}, bf16[24,3712]{1,0:T(8,128)(2,1)S(1)}, u32[]{:S(2)}, u32[]{:S(2)}) collective-permute-start(bf16[24,3712]{1,0:T(8,128)(2,1)S(1)} %add_convert_fusion.3), channel_id=1, source_target_pairs={{0,56},{1,9},{4,60},{5,13},{8,0},{9,17},{12,4},{13,21},{16,8},{17,... | collective-permute-start | bytes 534536 | tf_op jit(solution)/shard_map/ppermute | solution.py:23
  196.8 5.1 %collective-permute-done.29 = bf16[24,3712]{1,0:T(8,128)(2,1)S(1)} collective-permute-done((bf16[24,3712]{1,0:T(8,128)(2,1)S(1)}, bf16[24,3712]{1,0:T(8,128)(2,1)S(1)}, u32[]{:S(2)}, u32[]{:S(2)}) %collective-permute-start.29) | collective-permute-done | bytes 178208 | tf_op jit(solution)/shard_map/ppermute | solution.py:23
  202.0 1.9 collective-permute-start.34
  205.6 2.6 %collective-permute-start.35 = (bf16[1,12,3584]{2,1,0:T(8,128)(2,1)S(1)}, bf16[1,12,3584]{2,1,0:T(8,128)(2,1)S(1)}, u32[]{:S(2)}, u32[]{:S(2)}) collective-permute-start(bf16[1,12,3584]{2,1,0:T(8,128)(2,1)S(1)} %fusion.34), channel_id=1, source_target_pairs={{64,0},{128,64},{192,128},{256,192},{320,256},{384,320},{448,384},... | collective-permute-start | bytes 258056 | tf_op jit(solution)/shard_map/ppermute | solution.py:138
  209.0 7.2 %collective-permute-done.35 = bf16[1,12,3584]{2,1,0:T(8,128)(2,1)S(1)} collective-permute-done((bf16[1,12,3584]{2,1,0:T(8,128)(2,1)S(1)}, bf16[1,12,3584]{2,1,0:T(8,128)(2,1)S(1)}, u32[]{:S(2)}, u32[]{:S(2)}) %collective-permute-start.35) | collective-permute-done | bytes 86048 | tf_op jit(solution)/shard_map/ppermute | solution.py:138
  (99 shorter events, 32.0 us)
Async XLA Ops:
  0.6 29.4 %copy-start = (bf16[1,3584,256]{2,1,0:T(8,128)(2,1)S(1)}, bf16[1,3584,256]{2,1,0:T(8,128)(2,1)}, u32[]{:S(2)}) copy-start(bf16[1,3584,256]{2,1,0:T(8,128)(2,1)} %param.10) | copy-start | bytes 5505028
  3.4 12.6 %collective-permute-start.9 = (bf16[12,3712]{1,0:T(8,128)(2,1)S(1)}, bf16[12,3712]{1,0:T(8,128)(2,1)S(1)}, u32[]{:S(2)}, u32[]{:S(2)}) collective-permute-start(bf16[12,3712]{1,0:T(8,128)(2,1)S(1)} %pad_maximum_fusion.3), channel_id=1, source_target_pairs={{0,1},{1,0},{2,3},{3,2},{4,5},{5,4},{6,7},{7,6},{8,9},{9,8},{10,11... | collective-permute-start | bytes 267272 | tf_op jit(solution)/shard_map/ppermute | solution.py:13
  5.4 5.9 %collective-permute-start = (bf16[12,3584]{1,0:T(8,128)(2,1)}, bf16[12,3584]{1,0:T(8,128)(2,1)S(1)}, u32[]{:S(2)}, u32[]{:S(2)}) collective-permute-start(bf16[12,3584]{1,0:T(8,128)(2,1)} %bitcast.56), channel_id=1, source_target_pairs={{0,1},{1,0},{2,3},{3,2},{4,5},{5,4},{6,7},{7,6},{8,9},{9,8},{10,11... | collective-permute-start | bytes 258056 | tf_op jit(solution)/shard_map/ppermute | solution.py:13
  7.8 126.9 %collective-permute-start.20 = (bf16[256,3584]{1,0:T(8,128)(2,1)}, bf16[256,3584]{1,0:T(8,128)(2,1)}, u32[]{:S(2)}, u32[]{:S(2)}) collective-permute-start(bf16[256,3584]{1,0:T(8,128)(2,1)} %bitcast.60), channel_id=1, source_target_pairs={{0,2},{2,0},{1,3},{3,1},{4,6},{6,4},{5,7},{7,5},{8,10},{10,8},{9,1... | collective-permute-start | bytes 5505032 | tf_op jit(solution)/shard_map/ppermute | solution.py:13
  12.2 14.8 %collective-permute-start.1 = (bf16[24,3584]{1,0:T(8,128)(2,1)S(1)}, bf16[24,3584]{1,0:T(8,128)(2,1)S(1)}, u32[]{:S(2)}, u32[]{:S(2)}) collective-permute-start(bf16[24,3584]{1,0:T(8,128)(2,1)S(1)} %pad_maximum_fusion.2), channel_id=1, source_target_pairs={{0,4},{1,61},{4,8},{5,1},{8,12},{9,5},{12,16},{13,9},{16,20},{17,1... | collective-permute-start | bytes 516104 | tf_op jit(solution)/shard_map/ppermute | solution.py:23
  17.1 12.9 %collective-permute-start.10 = (bf16[24,3712]{1,0:T(8,128)(2,1)S(1)}, bf16[24,3712]{1,0:T(8,128)(2,1)S(1)}, u32[]{:S(2)}, u32[]{:S(2)}) collective-permute-start(bf16[24,3712]{1,0:T(8,128)(2,1)S(1)} %pad_maximum_fusion.1), channel_id=1, source_target_pairs={{0,4},{1,61},{4,8},{5,1},{8,12},{9,5},{12,16},{13,9},{16,20},{17,1... | collective-permute-start | bytes 534536 | tf_op jit(solution)/shard_map/ppermute | solution.py:23
  27.0 8.5 %collective-permute-start.2 = (bf16[24,3584]{1,0:T(8,128)(2,1)S(1)}, bf16[24,3584]{1,0:T(8,128)(2,1)S(1)}, u32[]{:S(2)}, u32[]{:S(2)}) collective-permute-start(bf16[24,3584]{1,0:T(8,128)(2,1)S(1)} %collective-permute-done.1), channel_id=1, source_target_pairs={{0,4},{1,61},{4,8},{5,1},{8,12},{9,5},{12,16},{13,9},{16,20},{17,1... | collective-permute-start | bytes 516104 | tf_op jit(solution)/shard_map/ppermute | solution.py:23
  30.1 86.8 %collective-permute-start.21 = (bf16[1792,256]{1,0:T(8,128)(2,1)S(1)}, bf16[1792,256]{1,0:T(8,128)(2,1)S(1)}, u32[]{:S(2)}, u32[]{:S(2)}) collective-permute-start(bf16[1792,256]{1,0:T(8,128)(2,1)S(1)} %slice.101), channel_id=1, source_target_pairs={{0,2},{2,0},{1,3},{3,1},{4,6},{6,4},{5,7},{7,5},{8,10},{10,8},{9,1... | collective-permute-start | bytes 2752520 | tf_op jit(solution)/shard_map/ppermute | solution.py:13
  32.5 8.6 %collective-permute-start.11 = (bf16[24,3712]{1,0:T(8,128)(2,1)S(1)}, bf16[24,3712]{1,0:T(8,128)(2,1)S(1)}, u32[]{:S(2)}, u32[]{:S(2)}) collective-permute-start(bf16[24,3712]{1,0:T(8,128)(2,1)S(1)} %collective-permute-done.10), channel_id=1, source_target_pairs={{0,4},{1,61},{4,8},{5,1},{8,12},{9,5},{12,16},{13,9},{16,20},{17,1... | collective-permute-start | bytes 534536 | tf_op jit(solution)/shard_map/ppermute | solution.py:23
  34.5 18.7 %copy-start.1 = (bf16[1,256,3584]{2,1,0:T(8,128)(2,1)S(1)}, bf16[1,256,3584]{2,1,0:T(8,128)(2,1)}, u32[]{:S(2)}) copy-start(bf16[1,256,3584]{2,1,0:T(8,128)(2,1)} %param.11) | copy-start | bytes 5505028
  35.5 11.0 %collective-permute-start.3 = (bf16[24,3584]{1,0:T(8,128)(2,1)S(1)}, bf16[24,3584]{1,0:T(8,128)(2,1)S(1)}, u32[]{:S(2)}, u32[]{:S(2)}) collective-permute-start(bf16[24,3584]{1,0:T(8,128)(2,1)S(1)} %collective-permute-done.2), channel_id=1, source_target_pairs={{0,4},{1,61},{4,8},{5,1},{8,12},{9,5},{12,16},{13,9},{16,20},{17,1... | collective-permute-start | bytes 516104 | tf_op jit(solution)/shard_map/ppermute | solution.py:23
  41.2 100.0 %collective-permute-start.22 = (bf16[1792,256]{1,0:T(8,128)(2,1)S(1)}, bf16[1792,256]{1,0:T(8,128)(2,1)S(1)}, u32[]{:S(2)}, u32[]{:S(2)}) collective-permute-start(bf16[1792,256]{1,0:T(8,128)(2,1)S(1)} %slice.102), channel_id=1, source_target_pairs={{0,2},{2,0},{1,3},{3,1},{4,6},{6,4},{5,7},{7,5},{8,10},{10,8},{9,1... | collective-permute-start | bytes 2752520 | tf_op jit(solution)/shard_map/ppermute | solution.py:13
  44.6 8.6 %collective-permute-start.12 = (bf16[24,3712]{1,0:T(8,128)(2,1)S(1)}, bf16[24,3712]{1,0:T(8,128)(2,1)S(1)}, u32[]{:S(2)}, u32[]{:S(2)}) collective-permute-start(bf16[24,3712]{1,0:T(8,128)(2,1)S(1)} %collective-permute-done.11), channel_id=1, source_target_pairs={{0,4},{1,61},{4,8},{5,1},{8,12},{9,5},{12,16},{13,9},{16,20},{17,1... | collective-permute-start | bytes 534536 | tf_op jit(solution)/shard_map/ppermute | solution.py:23
  46.6 8.6 %collective-permute-start.4 = (bf16[24,3584]{1,0:T(8,128)(2,1)S(1)}, bf16[24,3584]{1,0:T(8,128)(2,1)S(1)}, u32[]{:S(2)}, u32[]{:S(2)}) collective-permute-start(bf16[24,3584]{1,0:T(8,128)(2,1)S(1)} %collective-permute-done.3), channel_id=1, source_target_pairs={{0,4},{1,61},{4,8},{5,1},{8,12},{9,5},{12,16},{13,9},{16,20},{17,1... | collective-permute-start | bytes 516104 | tf_op jit(solution)/shard_map/ppermute | solution.py:23
  53.2 86.6 %collective-permute-start.18 = (bf16[256,3584]{1,0:T(8,128)(2,1)S(1)}, bf16[256,3584]{1,0:T(8,128)(2,1)S(1)}, u32[]{:S(2)}, u32[]{:S(2)}) collective-permute-start(bf16[256,3584]{1,0:T(8,128)(2,1)S(1)} %bitcast.61), channel_id=1, source_target_pairs={{0,1},{1,0},{2,3},{3,2},{4,5},{5,4},{6,7},{7,6},{8,9},{9,8},{10,11... | collective-permute-start | bytes 5505032 | tf_op jit(solution)/shard_map/ppermute | solution.py:13
  55.1 8.6 %collective-permute-start.13 = (bf16[24,3712]{1,0:T(8,128)(2,1)S(1)}, bf16[24,3712]{1,0:T(8,128)(2,1)S(1)}, u32[]{:S(2)}, u32[]{:S(2)}) collective-permute-start(bf16[24,3712]{1,0:T(8,128)(2,1)S(1)} %collective-permute-done.12), channel_id=1, source_target_pairs={{0,4},{1,61},{4,8},{5,1},{8,12},{9,5},{12,16},{13,9},{16,20},{17,1... | collective-permute-start | bytes 534536 | tf_op jit(solution)/shard_map/ppermute | solution.py:23
  63.7 8.5 %collective-permute-start.5 = (bf16[24,3584]{1,0:T(8,128)(2,1)S(1)}, bf16[24,3584]{1,0:T(8,128)(2,1)S(1)}, u32[]{:S(2)}, u32[]{:S(2)}) collective-permute-start(bf16[24,3584]{1,0:T(8,128)(2,1)S(1)} %collective-permute-done.4), channel_id=1, source_target_pairs={{0,4},{1,61},{4,8},{5,1},{8,12},{9,5},{12,16},{13,9},{16,20},{17,1... | collective-permute-start | bytes 516104 | tf_op jit(solution)/shard_map/ppermute | solution.py:23
  72.2 8.6 %collective-permute-start.14 = (bf16[24,3712]{1,0:T(8,128)(2,1)S(1)}, bf16[24,3712]{1,0:T(8,128)(2,1)S(1)}, u32[]{:S(2)}, u32[]{:S(2)}) collective-permute-start(bf16[24,3712]{1,0:T(8,128)(2,1)S(1)} %collective-permute-done.13), channel_id=1, source_target_pairs={{0,4},{1,61},{4,8},{5,1},{8,12},{9,5},{12,16},{13,9},{16,20},{17,1... | collective-permute-start | bytes 534536 | tf_op jit(solution)/shard_map/ppermute | solution.py:23
  80.8 8.5 %collective-permute-start.6 = (bf16[24,3584]{1,0:T(8,128)(2,1)S(1)}, bf16[24,3584]{1,0:T(8,128)(2,1)S(1)}, u32[]{:S(2)}, u32[]{:S(2)}) collective-permute-start(bf16[24,3584]{1,0:T(8,128)(2,1)S(1)} %collective-permute-done.5), channel_id=1, source_target_pairs={{0,4},{1,61},{4,8},{5,1},{8,12},{9,5},{12,16},{13,9},{16,20},{17,1... | collective-permute-start | bytes 516104 | tf_op jit(solution)/shard_map/ppermute | solution.py:23
  89.3 8.6 %collective-permute-start.15 = (bf16[24,3712]{1,0:T(8,128)(2,1)S(1)}, bf16[24,3712]{1,0:T(8,128)(2,1)S(1)}, u32[]{:S(2)}, u32[]{:S(2)}) collective-permute-start(bf16[24,3712]{1,0:T(8,128)(2,1)S(1)} %collective-permute-done.14), channel_id=1, source_target_pairs={{0,4},{1,61},{4,8},{5,1},{8,12},{9,5},{12,16},{13,9},{16,20},{17,1... | collective-permute-start | bytes 534536 | tf_op jit(solution)/shard_map/ppermute | solution.py:23
  97.8 8.5 %collective-permute-start.7 = (bf16[24,3584]{1,0:T(8,128)(2,1)S(1)}, bf16[24,3584]{1,0:T(8,128)(2,1)S(1)}, u32[]{:S(2)}, u32[]{:S(2)}) collective-permute-start(bf16[24,3584]{1,0:T(8,128)(2,1)S(1)} %collective-permute-done.6), channel_id=1, source_target_pairs={{0,4},{1,61},{4,8},{5,1},{8,12},{9,5},{12,16},{13,9},{16,20},{17,1... | collective-permute-start | bytes 516104 | tf_op jit(solution)/shard_map/ppermute | solution.py:23
  106.3 8.6 %collective-permute-start.16 = (bf16[24,3712]{1,0:T(8,128)(2,1)S(1)}, bf16[24,3712]{1,0:T(8,128)(2,1)S(1)}, u32[]{:S(2)}, u32[]{:S(2)}) collective-permute-start(bf16[24,3712]{1,0:T(8,128)(2,1)S(1)} %collective-permute-done.15), channel_id=1, source_target_pairs={{0,4},{1,61},{4,8},{5,1},{8,12},{9,5},{12,16},{13,9},{16,20},{17,1... | collective-permute-start | bytes 534536 | tf_op jit(solution)/shard_map/ppermute | solution.py:23
  114.9 8.5 %collective-permute-start.8 = (bf16[24,3584]{1,0:T(8,128)(2,1)S(1)}, bf16[24,3584]{1,0:T(8,128)(2,1)S(1)}, u32[]{:S(2)}, u32[]{:S(2)}) collective-permute-start(bf16[24,3584]{1,0:T(8,128)(2,1)S(1)} %collective-permute-done.7), channel_id=1, source_target_pairs={{0,4},{4,8},{8,12},{12,16},{16,20},{20,24},{24,28},{28,32},{32,36}... | collective-permute-start | bytes 516104 | tf_op jit(solution)/shard_map/ppermute | solution.py:23
  116.9 22.2 %collective-permute-start.19 = (bf16[3584,256]{1,0:T(8,128)(2,1)S(1)}, bf16[3584,256]{1,0:T(8,128)(2,1)S(1)}, u32[]{:S(2)}, u32[]{:S(2)}) collective-permute-start(bf16[3584,256]{1,0:T(8,128)(2,1)S(1)} %bitcast.53), channel_id=1, source_target_pairs={{0,1},{1,0},{2,3},{3,2},{4,5},{5,4},{6,7},{7,6},{8,9},{9,8},{10,11... | collective-permute-start | bytes 5505032 | tf_op jit(solution)/shard_map/ppermute | solution.py:13
  123.4 8.6 %collective-permute-start.17 = (bf16[24,3712]{1,0:T(8,128)(2,1)S(1)}, bf16[24,3712]{1,0:T(8,128)(2,1)S(1)}, u32[]{:S(2)}, u32[]{:S(2)}) collective-permute-start(bf16[24,3712]{1,0:T(8,128)(2,1)S(1)} %collective-permute-done.16), channel_id=1, source_target_pairs={{0,4},{4,8},{8,12},{12,16},{16,20},{20,24},{24,28},{28,32},{32,36}... | collective-permute-start | bytes 534536 | tf_op jit(solution)/shard_map/ppermute | solution.py:23
  132.0 14.6 %collective-permute-start.24 = (bf16[1792,256]{1,0:T(8,128)(2,1)S(1)}, bf16[1792,256]{1,0:T(8,128)(2,1)S(1)}, u32[]{:S(2)}, u32[]{:S(2)}) collective-permute-start(bf16[1792,256]{1,0:T(8,128)(2,1)S(1)} %collective-permute-done.21), channel_id=1, source_target_pairs={{0,1},{1,0},{2,3},{3,2},{4,5},{5,4},{6,7},{7,6},{8,9},{9,8},{10,11... | collective-permute-start | bytes 2752520 | tf_op jit(solution)/shard_map/ppermute | solution.py:13
  134.7 6.4 %collective-permute-start.23 = (bf16[256,3584]{1,0:T(8,128)(2,1)}, bf16[256,3584]{1,0:T(8,128)(2,1)S(1)}, u32[]{:S(2)}, u32[]{:S(2)}) collective-permute-start(bf16[256,3584]{1,0:T(8,128)(2,1)} %collective-permute-done.20), channel_id=1, source_target_pairs={{0,1},{1,0},{2,3},{3,2},{4,5},{5,4},{6,7},{7,6},{8,9},{9,8},{10,11... | collective-permute-start | bytes 5505032 | tf_op jit(solution)/shard_map/ppermute | solution.py:13
  141.2 5.5 %collective-permute-start.25 = (bf16[1792,256]{1,0:T(8,128)(2,1)S(1)}, bf16[1792,256]{1,0:T(8,128)(2,1)S(1)}, u32[]{:S(2)}, u32[]{:S(2)}) collective-permute-start(bf16[1792,256]{1,0:T(8,128)(2,1)S(1)} %collective-permute-done.22), channel_id=1, source_target_pairs={{0,1},{1,0},{2,3},{3,2},{4,5},{5,4},{6,7},{7,6},{8,9},{9,8},{10,11... | collective-permute-start | bytes 2752520 | tf_op jit(solution)/shard_map/ppermute | solution.py:13
  150.5 10.0 %collective-permute-start.26 = (bf16[24,3712]{1,0:T(8,128)(2,1)S(1)}, bf16[24,3712]{1,0:T(8,128)(2,1)S(1)}, u32[]{:S(2)}, u32[]{:S(2)}) collective-permute-start(bf16[24,3712]{1,0:T(8,128)(2,1)S(1)} %get-tuple-element.40), channel_id=1, source_target_pairs={{0,56},{4,60},{8,0},{12,4},{16,8},{20,12},{24,16},{28,20},{32,24},... | collective-permute-start | bytes 534536 | tf_op jit(solution)/shard_map/ppermute | solution.py:23
  152.7 14.0 %collective-permute-start.30 = (bf16[24,3712]{1,0:T(8,128)(2,1)S(1)}, bf16[24,3712]{1,0:T(8,128)(2,1)S(1)}, u32[]{:S(2)}, u32[]{:S(2)}) collective-permute-start(bf16[24,3712]{1,0:T(8,128)(2,1)S(1)} %get-tuple-element.36), channel_id=1, source_target_pairs={{0,56},{1,9},{4,60},{5,13},{8,0},{9,17},{12,4},{13,21},{16,8},{17,... | collective-permute-start | bytes 534536 | tf_op jit(solution)/shard_map/ppermute | solution.py:23
  160.6 12.8 %collective-permute-start.27 = (bf16[24,3712]{1,0:T(8,128)(2,1)S(1)}, bf16[24,3712]{1,0:T(8,128)(2,1)S(1)}, u32[]{:S(2)}, u32[]{:S(2)}) collective-permute-start(bf16[24,3712]{1,0:T(8,128)(2,1)S(1)} %add_convert_fusion.5), channel_id=1, source_target_pairs={{0,56},{1,9},{4,60},{5,13},{8,0},{9,17},{12,4},{13,21},{16,8},{17,... | collective-permute-start | bytes 534536 | tf_op jit(solution)/shard_map/ppermute | solution.py:23
  166.8 11.8 %collective-permute-start.31 = (bf16[24,3712]{1,0:T(8,128)(2,1)S(1)}, bf16[24,3712]{1,0:T(8,128)(2,1)S(1)}, u32[]{:S(2)}, u32[]{:S(2)}) collective-permute-start(bf16[24,3712]{1,0:T(8,128)(2,1)S(1)} %add_convert_fusion.2), channel_id=1, source_target_pairs={{0,56},{1,9},{4,60},{5,13},{8,0},{9,17},{12,4},{13,21},{16,8},{17,... | collective-permute-start | bytes 534536 | tf_op jit(solution)/shard_map/ppermute | solution.py:23
  173.4 11.7 %collective-permute-start.28 = (bf16[24,3712]{1,0:T(8,128)(2,1)S(1)}, bf16[24,3712]{1,0:T(8,128)(2,1)S(1)}, u32[]{:S(2)}, u32[]{:S(2)}) collective-permute-start(bf16[24,3712]{1,0:T(8,128)(2,1)S(1)} %add_convert_fusion.4), channel_id=1, source_target_pairs={{0,56},{1,9},{4,60},{5,13},{8,0},{9,17},{12,4},{13,21},{16,8},{17,... | collective-permute-start | bytes 534536 | tf_op jit(solution)/shard_map/ppermute | solution.py:23
  178.7 9.6 %collective-permute-start.32 = (bf16[24,3712]{1,0:T(8,128)(2,1)S(1)}, bf16[24,3712]{1,0:T(8,128)(2,1)S(1)}, u32[]{:S(2)}, u32[]{:S(2)}) collective-permute-start(bf16[24,3712]{1,0:T(8,128)(2,1)S(1)} %add_convert_fusion.1), channel_id=1, source_target_pairs={{0,56},{1,9},{4,60},{5,13},{8,0},{9,17},{12,4},{13,21},{16,8},{17,... | collective-permute-start | bytes 534536 | tf_op jit(solution)/shard_map/ppermute | solution.py:23
  188.3 8.4 %collective-permute-start.33 = (bf16[24,3712]{1,0:T(8,128)(2,1)S(1)}, bf16[24,3712]{1,0:T(8,128)(2,1)S(1)}, u32[]{:S(2)}, u32[]{:S(2)}) collective-permute-start(bf16[24,3712]{1,0:T(8,128)(2,1)S(1)} %add_convert_fusion), channel_id=1, source_target_pairs={{0,60},{1,5},{4,0},{5,9},{8,4},{9,13},{12,8},{13,17},{16,12},{17,2... | collective-permute-start | bytes 534536 | tf_op jit(solution)/shard_map/ppermute | solution.py:23
  192.0 9.9 %collective-permute-start.29 = (bf16[24,3712]{1,0:T(8,128)(2,1)S(1)}, bf16[24,3712]{1,0:T(8,128)(2,1)S(1)}, u32[]{:S(2)}, u32[]{:S(2)}) collective-permute-start(bf16[24,3712]{1,0:T(8,128)(2,1)S(1)} %add_convert_fusion.3), channel_id=1, source_target_pairs={{0,56},{1,9},{4,60},{5,13},{8,0},{9,17},{12,4},{13,21},{16,8},{17,... | collective-permute-start | bytes 534536 | tf_op jit(solution)/shard_map/ppermute | solution.py:23
  202.0 3.4 %collective-permute-start.34 = (f32[12,3712]{1,0:T(8,128)S(1)}, f32[12,3712]{1,0:T(8,128)S(1)}, u32[]{:S(2)}, u32[]{:S(2)}) collective-permute-start(f32[12,3712]{1,0:T(8,128)S(1)} %slice_select_fusion), channel_id=1, source_target_pairs={{0,1},{1,0},{2,3},{3,2},{4,5},{5,4},{6,7},{7,6},{8,9},{9,8},{10,11... | collective-permute-start | bytes 534536 | tf_op jit(solution)/shard_map/ppermute | solution.py:13
  205.6 10.7 %collective-permute-start.35 = (bf16[1,12,3584]{2,1,0:T(8,128)(2,1)S(1)}, bf16[1,12,3584]{2,1,0:T(8,128)(2,1)S(1)}, u32[]{:S(2)}, u32[]{:S(2)}) collective-permute-start(bf16[1,12,3584]{2,1,0:T(8,128)(2,1)S(1)} %fusion.34), channel_id=1, source_target_pairs={{64,0},{128,64},{192,128},{256,192},{320,256},{384,320},{448,384},... | collective-permute-start | bytes 258056 | tf_op jit(solution)/shard_map/ppermute | solution.py:138
where the time goes:
time: 218 us; the launch traced here: 217 us
  starting transfers between devices  99.6 us (46%)
  waiting for transfers between devices  96.5 us (44%)
  matrix products  11.6 us (5%)
  other arithmetic  4.3 us (2%)
  local copies, waits for them, and re-layouts  3.43 us (2%)
    ppermute x24, waiting for transfers between devices, along(): return lax.ppermute(block, ('z', 'c'), route)  87.8 us
    ppermute x24, starting transfers between devices, along(): return lax.ppermute(block, ('z', 'c'), route)  71.4 us
    ppermute x11, starting transfers between devices, swap(): return lax.ppermute(block, axis, [(0, 1), (1, 0)])  25.6 us
    dot_general x20, matrix products, dot(): lax.dot_general(left, right, (((left_dim,), (right_dim,)), ((), ())), pre...  11.6 us
    ppermute x1, waiting for transfers between devices, section(): lax.ppermute(grad_bf[None], 'pipe', [(i, i - 1) for i in range(1, section...  7.2 us
  transfers between devices with their start and end apart: 36, of which 20 were waited for; matrix products, arithmetic and copies ran while one was open for 5% of the time, Pallas kernels for 0%

commit v1 on v0

--- a/solution.py
+++ b/solution.py
@@ -55,7 +55,9 @@
         got = swap(rows, "c")
         return jnp.concatenate([jnp.where(first, rows, got), jnp.where(first, got, rows)], axis=0)
 
-    blocks = [beside(tailed), beside(upstream)]
+    packed_out = beside(upstream)
+    packed_in = beside(tailed)
+    blocks = [packed_in, packed_out]
 
     halves = lambda whole: (whole[:middle], whole[middle:])
     far_up, passed_up = [None, None], [None, None]
@@ -75,9 +77,8 @@
             near_down = swap(after(local_down, lead), "c")
         if step == 5:
             near_up = swap(after(local_up, lead), "c")
-        if step == 7:
+        if step == reach:
             passed_down = swap(after(far_down, lead), "c")
-        if step == reach:
             passed_up[0] = swap(after(far_up[0], lead), "c")
             passed_up[1] = swap(after(far_up[1], current[0], passed_down), "c")
             current = [jnp.where(first, chain, own) for chain, own in zip(current, blocks)]
@@ -127,7 +128,9 @@
         even = plus(along(even, -2, cores), parts[at]).astype(jnp.bfloat16)
         odd = plus(along(odd, -2), after(parts[at - 1], even)).astype(jnp.bfloat16)
     own = jnp.where(first, 0.0, parts[reach - 1].astype(jnp.float32))
-    carry = plus(along(even, -2), along(odd, -1)) + own
+    even = along(even, -2)
+    odd = along(odd, -1)
+    carry = plus(even, odd) + own
     keep = jnp.where(first, carry[:tok], carry[tok:])
     give = jnp.where(first, carry[tok:], carry[:tok])
     summed = keep + swap(give, "c")

time: 218 us -> 218 us (level)
  no operation moved by 1% of the time
where the time goes in v1:
time: 218 us; the launch traced here: 217 us
  starting transfers between devices  99.6 us (46%)
  waiting for transfers between devices  96.5 us (44%)
  matrix products  11.6 us (5%)
  other arithmetic  4.3 us (2%)
  local copies, waits for them, and re-layouts  3.43 us (2%)
    ppermute x24, waiting for transfers between devices, along(): return lax.ppermute(block, ('z', 'c'), route)  87.8 us
    ppermute x24, starting transfers between devices, along(): return lax.ppermute(block, ('z', 'c'), route)  71.4 us
    ppermute x11, starting transfers between devices, swap(): return lax.ppermute(block, axis, [(0, 1), (1, 0)])  25.6 us
    dot_general x20, matrix products, dot(): lax.dot_general(left, right, (((left_dim,), (right_dim,)), ((), ())), pre...  11.6 us
    ppermute x1, waiting for transfers between devices, section(): lax.ppermute(grad_bf[None], 'pipe', [(i, i - 1) for i in range(1, section...  7.2 us
  transfers between devices with their start and end apart: 36, of which 20 were waited for; matrix products, arithmetic and copies ran while one was open for 5% of the time, Pallas kernels for 0%

profile of v1, /device:TPU:24, one launch (start us, length us, event | category | flops | bytes accessed | tf_op | source)
XLA Modules:
  0.0 216.9 jit_solution(15694732735656600507)
XLA Ops:
  3.4 1.9 collective-permute-start.9
  5.4 2.4 %collective-permute-start = (bf16[12,3584]{1,0:T(8,128)(2,1)}, bf16[12,3584]{1,0:T(8,128)(2,1)S(1)}, u32[]{:S(2)}, u32[]{:S(2)}) collective-permute-start(bf16[12,3584]{1,0:T(8,128)(2,1)} %bitcast.56), channel_id=1, source_target_pairs={{0,1},{1,0},{2,3},{3,2},{4,5},{5,4},{6,7},{7,6},{8,9},{9,8},{10,11... | collective-permute-start | bytes 258056 | tf_op jit(solution)/shard_map/ppermute | solution.py:13
  7.8 3.4 %collective-permute-start.20 = (bf16[256,3584]{1,0:T(8,128)(2,1)}, bf16[256,3584]{1,0:T(8,128)(2,1)}, u32[]{:S(2)}, u32[]{:S(2)}) collective-permute-start(bf16[256,3584]{1,0:T(8,128)(2,1)} %bitcast.60), channel_id=1, source_target_pairs={{0,2},{2,0},{1,3},{3,1},{4,6},{6,4},{5,7},{7,5},{8,10},{10,8},{9,1... | collective-permute-start | bytes 5505032 | tf_op jit(solution)/shard_map/ppermute | solution.py:13
  12.2 3.8 %collective-permute-start.1 = (bf16[24,3584]{1,0:T(8,128)(2,1)S(1)}, bf16[24,3584]{1,0:T(8,128)(2,1)S(1)}, u32[]{:S(2)}, u32[]{:S(2)}) collective-permute-start(bf16[24,3584]{1,0:T(8,128)(2,1)S(1)} %pad_maximum_fusion.2), channel_id=1, source_target_pairs={{0,4},{1,61},{4,8},{5,1},{8,12},{9,5},{12,16},{13,9},{16,20},{17,1... | collective-permute-start | bytes 516104 | tf_op jit(solution)/shard_map/ppermute | solution.py:23
  17.1 3.8 %collective-permute-start.10 = (bf16[24,3712]{1,0:T(8,128)(2,1)S(1)}, bf16[24,3712]{1,0:T(8,128)(2,1)S(1)}, u32[]{:S(2)}, u32[]{:S(2)}) collective-permute-start(bf16[24,3712]{1,0:T(8,128)(2,1)S(1)} %pad_maximum_fusion.1), channel_id=1, source_target_pairs={{0,4},{1,61},{4,8},{5,1},{8,12},{9,5},{12,16},{13,9},{16,20},{17,1... | collective-permute-start | bytes 534536 | tf_op jit(solution)/shard_map/ppermute | solution.py:23
  20.9 6.1 %collective-permute-done.1 = bf16[24,3584]{1,0:T(8,128)(2,1)S(1)} collective-permute-done((bf16[24,3584]{1,0:T(8,128)(2,1)S(1)}, bf16[24,3584]{1,0:T(8,128)(2,1)S(1)}, u32[]{:S(2)}, u32[]{:S(2)}) %collective-permute-start.1) | collective-permute-done | bytes 172064 | tf_op jit(solution)/shard_map/ppermute | solution.py:23
  27.0 1.9 collective-permute-start.2
  30.1 2.4 %collective-permute-start.21 = (bf16[1792,256]{1,0:T(8,128)(2,1)S(1)}, bf16[1792,256]{1,0:T(8,128)(2,1)S(1)}, u32[]{:S(2)}, u32[]{:S(2)}) collective-permute-start(bf16[1792,256]{1,0:T(8,128)(2,1)S(1)} %slice.101), channel_id=1, source_target_pairs={{0,2},{2,0},{1,3},{3,1},{4,6},{6,4},{5,7},{7,5},{8,10},{10,8},{9,1... | collective-permute-start | bytes 2752520 | tf_op jit(solution)/shard_map/ppermute | solution.py:13
  32.5 1.9 collective-permute-start.11
  37.4 3.7 %collective-permute-done.11 = bf16[24,3712]{1,0:T(8,128)(2,1)S(1)} collective-permute-done((bf16[24,3712]{1,0:T(8,128)(2,1)S(1)}, bf16[24,3712]{1,0:T(8,128)(2,1)S(1)}, u32[]{:S(2)}, u32[]{:S(2)}) %collective-permute-start.11) | collective-permute-done | bytes 178208 | tf_op jit(solution)/shard_map/ppermute | solution.py:23
  41.2 3.4 %collective-permute-start.22 = (bf16[1792,256]{1,0:T(8,128)(2,1)S(1)}, bf16[1792,256]{1,0:T(8,128)(2,1)S(1)}, u32[]{:S(2)}, u32[]{:S(2)}) collective-permute-start(bf16[1792,256]{1,0:T(8,128)(2,1)S(1)} %slice.102), channel_id=1, source_target_pairs={{0,2},{2,0},{1,3},{3,1},{4,6},{6,4},{5,7},{7,5},{8,10},{10,8},{9,1... | collective-permute-start | bytes 2752520 | tf_op jit(solution)/shard_map/ppermute | solution.py:13
  44.6 1.9 collective-permute-start.12
  46.6 1.9 collective-permute-start.4
  48.5 4.7 %collective-permute-done.12 = bf16[24,3712]{1,0:T(8,128)(2,1)S(1)} collective-permute-done((bf16[24,3712]{1,0:T(8,128)(2,1)S(1)}, bf16[24,3712]{1,0:T(8,128)(2,1)S(1)}, u32[]{:S(2)}, u32[]{:S(2)}) %collective-permute-start.12) | collective-permute-done | bytes 178208 | tf_op jit(solution)/shard_map/ppermute | solution.py:23
  53.2 1.9 collective-permute-start.18
  55.1 1.9 collective-permute-start.13
  57.1 6.6 %collective-permute-done.13 = bf16[24,3712]{1,0:T(8,128)(2,1)S(1)} collective-permute-done((bf16[24,3712]{1,0:T(8,128)(2,1)S(1)}, bf16[24,3712]{1,0:T(8,128)(2,1)S(1)}, u32[]{:S(2)}, u32[]{:S(2)}) %collective-permute-start.13) | collective-permute-done | bytes 178208 | tf_op jit(solution)/shard_map/ppermute | solution.py:23
  63.7 1.9 collective-permute-start.5
  65.6 6.6 %collective-permute-done.5 = bf16[24,3584]{1,0:T(8,128)(2,1)S(1)} collective-permute-done((bf16[24,3584]{1,0:T(8,128)(2,1)S(1)}, bf16[24,3584]{1,0:T(8,128)(2,1)S(1)}, u32[]{:S(2)}, u32[]{:S(2)}) %collective-permute-start.5) | collective-permute-done | bytes 172064 | tf_op jit(solution)/shard_map/ppermute | solution.py:23
  72.2 1.9 collective-permute-start.14
  74.1 6.6 %collective-permute-done.14 = bf16[24,3712]{1,0:T(8,128)(2,1)S(1)} collective-permute-done((bf16[24,3712]{1,0:T(8,128)(2,1)S(1)}, bf16[24,3712]{1,0:T(8,128)(2,1)S(1)}, u32[]{:S(2)}, u32[]{:S(2)}) %collective-permute-start.14) | collective-permute-done | bytes 178208 | tf_op jit(solution)/shard_map/ppermute | solution.py:23
  82.7 6.6 %collective-permute-done.6 = bf16[24,3584]{1,0:T(8,128)(2,1)S(1)} collective-permute-done((bf16[24,3584]{1,0:T(8,128)(2,1)S(1)}, bf16[24,3584]{1,0:T(8,128)(2,1)S(1)}, u32[]{:S(2)}, u32[]{:S(2)}) %collective-permute-start.6) | collective-permute-done | bytes 172064 | tf_op jit(solution)/shard_map/ppermute | solution.py:23
  91.2 6.6 %collective-permute-done.15 = bf16[24,3712]{1,0:T(8,128)(2,1)S(1)} collective-permute-done((bf16[24,3712]{1,0:T(8,128)(2,1)S(1)}, bf16[24,3712]{1,0:T(8,128)(2,1)S(1)}, u32[]{:S(2)}, u32[]{:S(2)}) %collective-permute-start.15) | collective-permute-done | bytes 178208 | tf_op jit(solution)/shard_map/ppermute | solution.py:23
  97.8 1.9 collective-permute-start.7
  99.8 6.6 %collective-permute-done.7 = bf16[24,3584]{1,0:T(8,128)(2,1)S(1)} collective-permute-done((bf16[24,3584]{1,0:T(8,128)(2,1)S(1)}, bf16[24,3584]{1,0:T(8,128)(2,1)S(1)}, u32[]{:S(2)}, u32[]{:S(2)}) %collective-permute-start.7) | collective-permute-done | bytes 172064 | tf_op jit(solution)/shard_map/ppermute | solution.py:23
  106.3 1.9 collective-permute-start.16
  108.3 6.6 %collective-permute-done.16 = bf16[24,3712]{1,0:T(8,128)(2,1)S(1)} collective-permute-done((bf16[24,3712]{1,0:T(8,128)(2,1)S(1)}, bf16[24,3712]{1,0:T(8,128)(2,1)S(1)}, u32[]{:S(2)}, u32[]{:S(2)}) %collective-permute-start.16) | collective-permute-done | bytes 178208 | tf_op jit(solution)/shard_map/ppermute | solution.py:23
  116.9 1.9 collective-permute-start.19
  118.8 4.6 %collective-permute-done.8 = bf16[24,3584]{1,0:T(8,128)(2,1)S(1)} collective-permute-done((bf16[24,3584]{1,0:T(8,128)(2,1)S(1)}, bf16[24,3584]{1,0:T(8,128)(2,1)S(1)}, u32[]{:S(2)}, u32[]{:S(2)}) %collective-permute-start.8) | collective-permute-done | bytes 172064 | tf_op jit(solution)/shard_map/ppermute | solution.py:23
  125.4 6.6 %collective-permute-done.17 = bf16[24,3712]{1,0:T(8,128)(2,1)S(1)} collective-permute-done((bf16[24,3712]{1,0:T(8,128)(2,1)S(1)}, bf16[24,3712]{1,0:T(8,128)(2,1)S(1)}, u32[]{:S(2)}, u32[]{:S(2)}) %collective-permute-start.17) | collective-permute-done | bytes 178208 | tf_op jit(solution)/shard_map/ppermute | solution.py:23
  134.7 2.4 %collective-permute-start.23 = (bf16[256,3584]{1,0:T(8,128)(2,1)}, bf16[256,3584]{1,0:T(8,128)(2,1)S(1)}, u32[]{:S(2)}, u32[]{:S(2)}) collective-permute-start(bf16[256,3584]{1,0:T(8,128)(2,1)} %collective-permute-done.20), channel_id=1, source_target_pairs={{0,1},{1,0},{2,3},{3,2},{4,5},{5,4},{6,7},{7,6},{8,9},{9,8},{10,11... | collective-permute-start | bytes 5505032 | tf_op jit(solution)/shard_map/ppermute | solution.py:13
  141.2 1.9 collective-permute-start.25
  144.3 2.3 %multiply_convert_fusion.1 = (bf16[192,256]{1,0:T(8,128)(2,1)S(1)}, f32[192]{0:T(256)S(1)}) fusion(f32[192,256]{1,0:T(8,128)S(1)} %convolution_add_fusion.3, bf16[192,3584]{1,0:T(8,128)(2,1)S(1)} %select_dynamic-update-slice_fusion.1, bf16[256,3584]{1,0:T(8,128)(2,1)} %collective-permute-done.20), kind=kOutput, calls=%fused_computation.55 | convolution fusion | flops 352911168 | bytes 3506944 | tf_op jit(solution)/shard_map/dot_general | solution.py:91
  150.5 2.2 collective-permute-start.26
  152.7 7.8 %collective-permute-start.30 = (bf16[24,3712]{1,0:T(8,128)(2,1)S(1)}, bf16[24,3712]{1,0:T(8,128)(2,1)S(1)}, u32[]{:S(2)}, u32[]{:S(2)}) collective-permute-start(bf16[24,3712]{1,0:T(8,128)(2,1)S(1)} %get-tuple-element.36), channel_id=1, source_target_pairs={{0,56},{1,9},{4,60},{5,13},{8,0},{9,17},{12,4},{13,21},{16,8},{17,... | collective-permute-start | bytes 534536 | tf_op jit(solution)/shard_map/ppermute | solution.py:23
  160.6 3.7 %collective-permute-start.27 = (bf16[24,3712]{1,0:T(8,128)(2,1)S(1)}, bf16[24,3712]{1,0:T(8,128)(2,1)S(1)}, u32[]{:S(2)}, u32[]{:S(2)}) collective-permute-start(bf16[24,3712]{1,0:T(8,128)(2,1)S(1)} %add_convert_fusion.5), channel_id=1, source_target_pairs={{0,56},{1,9},{4,60},{5,13},{8,0},{9,17},{12,4},{13,21},{16,8},{17,... | collective-permute-start | bytes 534536 | tf_op jit(solution)/shard_map/ppermute | solution.py:23
  164.3 2.5 %collective-permute-done.30 = bf16[24,3712]{1,0:T(8,128)(2,1)S(1)} collective-permute-done((bf16[24,3712]{1,0:T(8,128)(2,1)S(1)}, bf16[24,3712]{1,0:T(8,128)(2,1)S(1)}, u32[]{:S(2)}, u32[]{:S(2)}) %collective-permute-start.30) | collective-permute-done | bytes 178208 | tf_op jit(solution)/shard_map/ppermute | solution.py:23
  166.8 6.6 %collective-permute-start.31 = (bf16[24,3712]{1,0:T(8,128)(2,1)S(1)}, bf16[24,3712]{1,0:T(8,128)(2,1)S(1)}, u32[]{:S(2)}, u32[]{:S(2)}) collective-permute-start(bf16[24,3712]{1,0:T(8,128)(2,1)S(1)} %add_convert_fusion.2), channel_id=1, source_target_pairs={{0,56},{1,9},{4,60},{5,13},{8,0},{9,17},{12,4},{13,21},{16,8},{17,... | collective-permute-start | bytes 534536 | tf_op jit(solution)/shard_map/ppermute | solution.py:23
  173.4 1.9 collective-permute-start.28
  175.4 3.2 %collective-permute-done.31 = bf16[24,3712]{1,0:T(8,128)(2,1)S(1)} collective-permute-done((bf16[24,3712]{1,0:T(8,128)(2,1)S(1)}, bf16[24,3712]{1,0:T(8,128)(2,1)S(1)}, u32[]{:S(2)}, u32[]{:S(2)}) %collective-permute-start.31) | collective-permute-done | bytes 178208 | tf_op jit(solution)/shard_map/ppermute | solution.py:23
  178.7 6.5 %collective-permute-start.32 = (bf16[24,3712]{1,0:T(8,128)(2,1)S(1)}, bf16[24,3712]{1,0:T(8,128)(2,1)S(1)}, u32[]{:S(2)}, u32[]{:S(2)}) collective-permute-start(bf16[24,3712]{1,0:T(8,128)(2,1)S(1)} %add_convert_fusion.1), channel_id=1, source_target_pairs={{0,56},{1,9},{4,60},{5,13},{8,0},{9,17},{12,4},{13,21},{16,8},{17,... | collective-permute-start | bytes 534536 | tf_op jit(solution)/shard_map/ppermute | solution.py:23
  185.2 3.1 %collective-permute-done.32 = bf16[24,3712]{1,0:T(8,128)(2,1)S(1)} collective-permute-done((bf16[24,3712]{1,0:T(8,128)(2,1)S(1)}, bf16[24,3712]{1,0:T(8,128)(2,1)S(1)}, u32[]{:S(2)}, u32[]{:S(2)}) %collective-permute-start.32) | collective-permute-done | bytes 178208 | tf_op jit(solution)/shard_map/ppermute | solution.py:23
  188.3 3.7 %collective-permute-start.33 = (bf16[24,3712]{1,0:T(8,128)(2,1)S(1)}, bf16[24,3712]{1,0:T(8,128)(2,1)S(1)}, u32[]{:S(2)}, u32[]{:S(2)}) collective-permute-start(bf16[24,3712]{1,0:T(8,128)(2,1)S(1)} %add_convert_fusion), channel_id=1, source_target_pairs={{0,60},{1,5},{4,0},{5,9},{8,4},{9,13},{12,8},{13,17},{16,12},{17,2... | collective-permute-start | bytes 534536 | tf_op jit(solution)/shard_map/ppermute | solution.py:23
  192.0 4.7 %collective-permute-start.29 = (bf16[24,3712]{1,0:T(8,128)(2,1)S(1)}, bf16[24,3712]{1,0:T(8,128)(2,1)S(1)}, u32[]{:S(2)}, u32[]{:S(2)}) collective-permute-start(bf16[24,3712]{1,0:T(8,128)(2,1)S(1)} %add_convert_fusion.3), channel_id=1, source_target_pairs={{0,56},{1,9},{4,60},{5,13},{8,0},{9,17},{12,4},{13,21},{16,8},{17,... | collective-permute-start | bytes 534536 | tf_op jit(solution)/shard_map/ppermute | solution.py:23
  196.8 5.1 %collective-permute-done.29 = bf16[24,3712]{1,0:T(8,128)(2,1)S(1)} collective-permute-done((bf16[24,3712]{1,0:T(8,128)(2,1)S(1)}, bf16[24,3712]{1,0:T(8,128)(2,1)S(1)}, u32[]{:S(2)}, u32[]{:S(2)}) %collective-permute-start.29) | collective-permute-done | bytes 178208 | tf_op jit(solution)/shard_map/ppermute | solution.py:23
  202.0 1.9 collective-permute-start.34
  205.6 2.6 %collective-permute-start.35 = (bf16[1,12,3584]{2,1,0:T(8,128)(2,1)S(1)}, bf16[1,12,3584]{2,1,0:T(8,128)(2,1)S(1)}, u32[]{:S(2)}, u32[]{:S(2)}) collective-permute-start(bf16[1,12,3584]{2,1,0:T(8,128)(2,1)S(1)} %fusion.34), channel_id=1, source_target_pairs={{64,0},{128,64},{192,128},{256,192},{320,256},{384,320},{448,384},... | collective-permute-start | bytes 258056 | tf_op jit(solution)/shard_map/ppermute | solution.py:141
  209.0 7.2 %collective-permute-done.35 = bf16[1,12,3584]{2,1,0:T(8,128)(2,1)S(1)} collective-permute-done((bf16[1,12,3584]{2,1,0:T(8,128)(2,1)S(1)}, bf16[1,12,3584]{2,1,0:T(8,128)(2,1)S(1)}, u32[]{:S(2)}, u32[]{:S(2)}) %collective-permute-start.35) | collective-permute-done | bytes 86048 | tf_op jit(solution)/shard_map/ppermute | solution.py:141
  (99 shorter events, 32.0 us)
Async XLA Ops:
  0.6 29.4 %copy-start = (bf16[1,3584,256]{2,1,0:T(8,128)(2,1)S(1)}, bf16[1,3584,256]{2,1,0:T(8,128)(2,1)}, u32[]{:S(2)}) copy-start(bf16[1,3584,256]{2,1,0:T(8,128)(2,1)} %param.10) | copy-start | bytes 5505028
  3.4 12.6 %collective-permute-start.9 = (bf16[12,3712]{1,0:T(8,128)(2,1)S(1)}, bf16[12,3712]{1,0:T(8,128)(2,1)S(1)}, u32[]{:S(2)}, u32[]{:S(2)}) collective-permute-start(bf16[12,3712]{1,0:T(8,128)(2,1)S(1)} %pad_maximum_fusion.3), channel_id=1, source_target_pairs={{0,1},{1,0},{2,3},{3,2},{4,5},{5,4},{6,7},{7,6},{8,9},{9,8},{10,11... | collective-permute-start | bytes 267272 | tf_op jit(solution)/shard_map/ppermute | solution.py:13
  5.4 5.9 %collective-permute-start = (bf16[12,3584]{1,0:T(8,128)(2,1)}, bf16[12,3584]{1,0:T(8,128)(2,1)S(1)}, u32[]{:S(2)}, u32[]{:S(2)}) collective-permute-start(bf16[12,3584]{1,0:T(8,128)(2,1)} %bitcast.56), channel_id=1, source_target_pairs={{0,1},{1,0},{2,3},{3,2},{4,5},{5,4},{6,7},{7,6},{8,9},{9,8},{10,11... | collective-permute-start | bytes 258056 | tf_op jit(solution)/shard_map/ppermute | solution.py:13
  7.8 126.9 %collective-permute-start.20 = (bf16[256,3584]{1,0:T(8,128)(2,1)}, bf16[256,3584]{1,0:T(8,128)(2,1)}, u32[]{:S(2)}, u32[]{:S(2)}) collective-permute-start(bf16[256,3584]{1,0:T(8,128)(2,1)} %bitcast.60), channel_id=1, source_target_pairs={{0,2},{2,0},{1,3},{3,1},{4,6},{6,4},{5,7},{7,5},{8,10},{10,8},{9,1... | collective-permute-start | bytes 5505032 | tf_op jit(solution)/shard_map/ppermute | solution.py:13
  12.2 14.8 %collective-permute-start.1 = (bf16[24,3584]{1,0:T(8,128)(2,1)S(1)}, bf16[24,3584]{1,0:T(8,128)(2,1)S(1)}, u32[]{:S(2)}, u32[]{:S(2)}) collective-permute-start(bf16[24,3584]{1,0:T(8,128)(2,1)S(1)} %pad_maximum_fusion.2), channel_id=1, source_target_pairs={{0,4},{1,61},{4,8},{5,1},{8,12},{9,5},{12,16},{13,9},{16,20},{17,1... | collective-permute-start | bytes 516104 | tf_op jit(solution)/shard_map/ppermute | solution.py:23
  17.1 12.9 %collective-permute-start.10 = (bf16[24,3712]{1,0:T(8,128)(2,1)S(1)}, bf16[24,3712]{1,0:T(8,128)(2,1)S(1)}, u32[]{:S(2)}, u32[]{:S(2)}) collective-permute-start(bf16[24,3712]{1,0:T(8,128)(2,1)S(1)} %pad_maximum_fusion.1), channel_id=1, source_target_pairs={{0,4},{1,61},{4,8},{5,1},{8,12},{9,5},{12,16},{13,9},{16,20},{17,1... | collective-permute-start | bytes 534536 | tf_op jit(solution)/shard_map/ppermute | solution.py:23
  27.0 8.5 %collective-permute-start.2 = (bf16[24,3584]{1,0:T(8,128)(2,1)S(1)}, bf16[24,3584]{1,0:T(8,128)(2,1)S(1)}, u32[]{:S(2)}, u32[]{:S(2)}) collective-permute-start(bf16[24,3584]{1,0:T(8,128)(2,1)S(1)} %collective-permute-done.1), channel_id=1, source_target_pairs={{0,4},{1,61},{4,8},{5,1},{8,12},{9,5},{12,16},{13,9},{16,20},{17,1... | collective-permute-start | bytes 516104 | tf_op jit(solution)/shard_map/ppermute | solution.py:23
  30.1 86.8 %collective-permute-start.21 = (bf16[1792,256]{1,0:T(8,128)(2,1)S(1)}, bf16[1792,256]{1,0:T(8,128)(2,1)S(1)}, u32[]{:S(2)}, u32[]{:S(2)}) collective-permute-start(bf16[1792,256]{1,0:T(8,128)(2,1)S(1)} %slice.101), channel_id=1, source_target_pairs={{0,2},{2,0},{1,3},{3,1},{4,6},{6,4},{5,7},{7,5},{8,10},{10,8},{9,1... | collective-permute-start | bytes 2752520 | tf_op jit(solution)/shard_map/ppermute | solution.py:13
  32.5 8.6 %collective-permute-start.11 = (bf16[24,3712]{1,0:T(8,128)(2,1)S(1)}, bf16[24,3712]{1,0:T(8,128)(2,1)S(1)}, u32[]{:S(2)}, u32[]{:S(2)}) collective-permute-start(bf16[24,3712]{1,0:T(8,128)(2,1)S(1)} %collective-permute-done.10), channel_id=1, source_target_pairs={{0,4},{1,61},{4,8},{5,1},{8,12},{9,5},{12,16},{13,9},{16,20},{17,1... | collective-permute-start | bytes 534536 | tf_op jit(solution)/shard_map/ppermute | solution.py:23
  34.5 18.7 %copy-start.1 = (bf16[1,256,3584]{2,1,0:T(8,128)(2,1)S(1)}, bf16[1,256,3584]{2,1,0:T(8,128)(2,1)}, u32[]{:S(2)}) copy-start(bf16[1,256,3584]{2,1,0:T(8,128)(2,1)} %param.11) | copy-start | bytes 5505028
  35.5 11.0 %collective-permute-start.3 = (bf16[24,3584]{1,0:T(8,128)(2,1)S(1)}, bf16[24,3584]{1,0:T(8,128)(2,1)S(1)}, u32[]{:S(2)}, u32[]{:S(2)}) collective-permute-start(bf16[24,3584]{1,0:T(8,128)(2,1)S(1)} %collective-permute-done.2), channel_id=1, source_target_pairs={{0,4},{1,61},{4,8},{5,1},{8,12},{9,5},{12,16},{13,9},{16,20},{17,1... | collective-permute-start | bytes 516104 | tf_op jit(solution)/shard_map/ppermute | solution.py:23
  41.2 100.0 %collective-permute-start.22 = (bf16[1792,256]{1,0:T(8,128)(2,1)S(1)}, bf16[1792,256]{1,0:T(8,128)(2,1)S(1)}, u32[]{:S(2)}, u32[]{:S(2)}) collective-permute-start(bf16[1792,256]{1,0:T(8,128)(2,1)S(1)} %slice.102), channel_id=1, source_target_pairs={{0,2},{2,0},{1,3},{3,1},{4,6},{6,4},{5,7},{7,5},{8,10},{10,8},{9,1... | collective-permute-start | bytes 2752520 | tf_op jit(solution)/shard_map/ppermute | solution.py:13
  44.6 8.6 %collective-permute-start.12 = (bf16[24,3712]{1,0:T(8,128)(2,1)S(1)}, bf16[24,3712]{1,0:T(8,128)(2,1)S(1)}, u32[]{:S(2)}, u32[]{:S(2)}) collective-permute-start(bf16[24,3712]{1,0:T(8,128)(2,1)S(1)} %collective-permute-done.11), channel_id=1, source_target_pairs={{0,4},{1,61},{4,8},{5,1},{8,12},{9,5},{12,16},{13,9},{16,20},{17,1... | collective-permute-start | bytes 534536 | tf_op jit(solution)/shard_map/ppermute | solution.py:23
  46.6 8.6 %collective-permute-start.4 = (bf16[24,3584]{1,0:T(8,128)(2,1)S(1)}, bf16[24,3584]{1,0:T(8,128)(2,1)S(1)}, u32[]{:S(2)}, u32[]{:S(2)}) collective-permute-start(bf16[24,3584]{1,0:T(8,128)(2,1)S(1)} %collective-permute-done.3), channel_id=1, source_target_pairs={{0,4},{1,61},{4,8},{5,1},{8,12},{9,5},{12,16},{13,9},{16,20},{17,1... | collective-permute-start | bytes 516104 | tf_op jit(solution)/shard_map/ppermute | solution.py:23
  53.2 86.6 %collective-permute-start.18 = (bf16[256,3584]{1,0:T(8,128)(2,1)S(1)}, bf16[256,3584]{1,0:T(8,128)(2,1)S(1)}, u32[]{:S(2)}, u32[]{:S(2)}) collective-permute-start(bf16[256,3584]{1,0:T(8,128)(2,1)S(1)} %bitcast.61), channel_id=1, source_target_pairs={{0,1},{1,0},{2,3},{3,2},{4,5},{5,4},{6,7},{7,6},{8,9},{9,8},{10,11... | collective-permute-start | bytes 5505032 | tf_op jit(solution)/shard_map/ppermute | solution.py:13
  55.1 8.6 %collective-permute-start.13 = (bf16[24,3712]{1,0:T(8,128)(2,1)S(1)}, bf16[24,3712]{1,0:T(8,128)(2,1)S(1)}, u32[]{:S(2)}, u32[]{:S(2)}) collective-permute-start(bf16[24,3712]{1,0:T(8,128)(2,1)S(1)} %collective-permute-done.12), channel_id=1, source_target_pairs={{0,4},{1,61},{4,8},{5,1},{8,12},{9,5},{12,16},{13,9},{16,20},{17,1... | collective-permute-start | bytes 534536 | tf_op jit(solution)/shard_map/ppermute | solution.py:23
  63.7 8.5 %collective-permute-start.5 = (bf16[24,3584]{1,0:T(8,128)(2,1)S(1)}, bf16[24,3584]{1,0:T(8,128)(2,1)S(1)}, u32[]{:S(2)}, u32[]{:S(2)}) collective-permute-start(bf16[24,3584]{1,0:T(8,128)(2,1)S(1)} %collective-permute-done.4), channel_id=1, source_target_pairs={{0,4},{1,61},{4,8},{5,1},{8,12},{9,5},{12,16},{13,9},{16,20},{17,1... | collective-permute-start | bytes 516104 | tf_op jit(solution)/shard_map/ppermute | solution.py:23
  72.2 8.6 %collective-permute-start.14 = (bf16[24,3712]{1,0:T(8,128)(2,1)S(1)}, bf16[24,3712]{1,0:T(8,128)(2,1)S(1)}, u32[]{:S(2)}, u32[]{:S(2)}) collective-permute-start(bf16[24,3712]{1,0:T(8,128)(2,1)S(1)} %collective-permute-done.13), channel_id=1, source_target_pairs={{0,4},{1,61},{4,8},{5,1},{8,12},{9,5},{12,16},{13,9},{16,20},{17,1... | collective-permute-start | bytes 534536 | tf_op jit(solution)/shard_map/ppermute | solution.py:23
  80.8 8.5 %collective-permute-start.6 = (bf16[24,3584]{1,0:T(8,128)(2,1)S(1)}, bf16[24,3584]{1,0:T(8,128)(2,1)S(1)}, u32[]{:S(2)}, u32[]{:S(2)}) collective-permute-start(bf16[24,3584]{1,0:T(8,128)(2,1)S(1)} %collective-permute-done.5), channel_id=1, source_target_pairs={{0,4},{1,61},{4,8},{5,1},{8,12},{9,5},{12,16},{13,9},{16,20},{17,1... | collective-permute-start | bytes 516104 | tf_op jit(solution)/shard_map/ppermute | solution.py:23
  89.3 8.6 %collective-permute-start.15 = (bf16[24,3712]{1,0:T(8,128)(2,1)S(1)}, bf16[24,3712]{1,0:T(8,128)(2,1)S(1)}, u32[]{:S(2)}, u32[]{:S(2)}) collective-permute-start(bf16[24,3712]{1,0:T(8,128)(2,1)S(1)} %collective-permute-done.14), channel_id=1, source_target_pairs={{0,4},{1,61},{4,8},{5,1},{8,12},{9,5},{12,16},{13,9},{16,20},{17,1... | collective-permute-start | bytes 534536 | tf_op jit(solution)/shard_map/ppermute | solution.py:23
  97.8 8.5 %collective-permute-start.7 = (bf16[24,3584]{1,0:T(8,128)(2,1)S(1)}, bf16[24,3584]{1,0:T(8,128)(2,1)S(1)}, u32[]{:S(2)}, u32[]{:S(2)}) collective-permute-start(bf16[24,3584]{1,0:T(8,128)(2,1)S(1)} %collective-permute-done.6), channel_id=1, source_target_pairs={{0,4},{1,61},{4,8},{5,1},{8,12},{9,5},{12,16},{13,9},{16,20},{17,1... | collective-permute-start | bytes 516104 | tf_op jit(solution)/shard_map/ppermute | solution.py:23
  106.3 8.6 %collective-permute-start.16 = (bf16[24,3712]{1,0:T(8,128)(2,1)S(1)}, bf16[24,3712]{1,0:T(8,128)(2,1)S(1)}, u32[]{:S(2)}, u32[]{:S(2)}) collective-permute-start(bf16[24,3712]{1,0:T(8,128)(2,1)S(1)} %collective-permute-done.15), channel_id=1, source_target_pairs={{0,4},{1,61},{4,8},{5,1},{8,12},{9,5},{12,16},{13,9},{16,20},{17,1... | collective-permute-start | bytes 534536 | tf_op jit(solution)/shard_map/ppermute | solution.py:23
  114.9 8.5 %collective-permute-start.8 = (bf16[24,3584]{1,0:T(8,128)(2,1)S(1)}, bf16[24,3584]{1,0:T(8,128)(2,1)S(1)}, u32[]{:S(2)}, u32[]{:S(2)}) collective-permute-start(bf16[24,3584]{1,0:T(8,128)(2,1)S(1)} %collective-permute-done.7), channel_id=1, source_target_pairs={{0,4},{4,8},{8,12},{12,16},{16,20},{20,24},{24,28},{28,32},{32,36}... | collective-permute-start | bytes 516104 | tf_op jit(solution)/shard_map/ppermute | solution.py:23
  116.9 22.2 %collective-permute-start.19 = (bf16[3584,256]{1,0:T(8,128)(2,1)S(1)}, bf16[3584,256]{1,0:T(8,128)(2,1)S(1)}, u32[]{:S(2)}, u32[]{:S(2)}) collective-permute-start(bf16[3584,256]{1,0:T(8,128)(2,1)S(1)} %bitcast.53), channel_id=1, source_target_pairs={{0,1},{1,0},{2,3},{3,2},{4,5},{5,4},{6,7},{7,6},{8,9},{9,8},{10,11... | collective-permute-start | bytes 5505032 | tf_op jit(solution)/shard_map/ppermute | solution.py:13
  123.4 8.6 %collective-permute-start.17 = (bf16[24,3712]{1,0:T(8,128)(2,1)S(1)}, bf16[24,3712]{1,0:T(8,128)(2,1)S(1)}, u32[]{:S(2)}, u32[]{:S(2)}) collective-permute-start(bf16[24,3712]{1,0:T(8,128)(2,1)S(1)} %collective-permute-done.16), channel_id=1, source_target_pairs={{0,4},{4,8},{8,12},{12,16},{16,20},{20,24},{24,28},{28,32},{32,36}... | collective-permute-start | bytes 534536 | tf_op jit(solution)/shard_map/ppermute | solution.py:23
  132.0 14.6 %collective-permute-start.24 = (bf16[1792,256]{1,0:T(8,128)(2,1)S(1)}, bf16[1792,256]{1,0:T(8,128)(2,1)S(1)}, u32[]{:S(2)}, u32[]{:S(2)}) collective-permute-start(bf16[1792,256]{1,0:T(8,128)(2,1)S(1)} %collective-permute-done.21), channel_id=1, source_target_pairs={{0,1},{1,0},{2,3},{3,2},{4,5},{5,4},{6,7},{7,6},{8,9},{9,8},{10,11... | collective-permute-start | bytes 2752520 | tf_op jit(solution)/shard_map/ppermute | solution.py:13
  134.7 6.4 %collective-permute-start.23 = (bf16[256,3584]{1,0:T(8,128)(2,1)}, bf16[256,3584]{1,0:T(8,128)(2,1)S(1)}, u32[]{:S(2)}, u32[]{:S(2)}) collective-permute-start(bf16[256,3584]{1,0:T(8,128)(2,1)} %collective-permute-done.20), channel_id=1, source_target_pairs={{0,1},{1,0},{2,3},{3,2},{4,5},{5,4},{6,7},{7,6},{8,9},{9,8},{10,11... | collective-permute-start | bytes 5505032 | tf_op jit(solution)/shard_map/ppermute | solution.py:13
  141.2 5.5 %collective-permute-start.25 = (bf16[1792,256]{1,0:T(8,128)(2,1)S(1)}, bf16[1792,256]{1,0:T(8,128)(2,1)S(1)}, u32[]{:S(2)}, u32[]{:S(2)}) collective-permute-start(bf16[1792,256]{1,0:T(8,128)(2,1)S(1)} %collective-permute-done.22), channel_id=1, source_target_pairs={{0,1},{1,0},{2,3},{3,2},{4,5},{5,4},{6,7},{7,6},{8,9},{9,8},{10,11... | collective-permute-start | bytes 2752520 | tf_op jit(solution)/shard_map/ppermute | solution.py:13
  150.5 10.0 %collective-permute-start.26 = (bf16[24,3712]{1,0:T(8,128)(2,1)S(1)}, bf16[24,3712]{1,0:T(8,128)(2,1)S(1)}, u32[]{:S(2)}, u32[]{:S(2)}) collective-permute-start(bf16[24,3712]{1,0:T(8,128)(2,1)S(1)} %get-tuple-element.40), channel_id=1, source_target_pairs={{0,56},{4,60},{8,0},{12,4},{16,8},{20,12},{24,16},{28,20},{32,24},... | collective-permute-start | bytes 534536 | tf_op jit(solution)/shard_map/ppermute | solution.py:23
  152.7 14.0 %collective-permute-start.30 = (bf16[24,3712]{1,0:T(8,128)(2,1)S(1)}, bf16[24,3712]{1,0:T(8,128)(2,1)S(1)}, u32[]{:S(2)}, u32[]{:S(2)}) collective-permute-start(bf16[24,3712]{1,0:T(8,128)(2,1)S(1)} %get-tuple-element.36), channel_id=1, source_target_pairs={{0,56},{1,9},{4,60},{5,13},{8,0},{9,17},{12,4},{13,21},{16,8},{17,... | collective-permute-start | bytes 534536 | tf_op jit(solution)/shard_map/ppermute | solution.py:23
  160.6 12.8 %collective-permute-start.27 = (bf16[24,3712]{1,0:T(8,128)(2,1)S(1)}, bf16[24,3712]{1,0:T(8,128)(2,1)S(1)}, u32[]{:S(2)}, u32[]{:S(2)}) collective-permute-start(bf16[24,3712]{1,0:T(8,128)(2,1)S(1)} %add_convert_fusion.5), channel_id=1, source_target_pairs={{0,56},{1,9},{4,60},{5,13},{8,0},{9,17},{12,4},{13,21},{16,8},{17,... | collective-permute-start | bytes 534536 | tf_op jit(solution)/shard_map/ppermute | solution.py:23
  166.8 11.8 %collective-permute-start.31 = (bf16[24,3712]{1,0:T(8,128)(2,1)S(1)}, bf16[24,3712]{1,0:T(8,128)(2,1)S(1)}, u32[]{:S(2)}, u32[]{:S(2)}) collective-permute-start(bf16[24,3712]{1,0:T(8,128)(2,1)S(1)} %add_convert_fusion.2), channel_id=1, source_target_pairs={{0,56},{1,9},{4,60},{5,13},{8,0},{9,17},{12,4},{13,21},{16,8},{17,... | collective-permute-start | bytes 534536 | tf_op jit(solution)/shard_map/ppermute | solution.py:23
  173.4 11.7 %collective-permute-start.28 = (bf16[24,3712]{1,0:T(8,128)(2,1)S(1)}, bf16[24,3712]{1,0:T(8,128)(2,1)S(1)}, u32[]{:S(2)}, u32[]{:S(2)}) collective-permute-start(bf16[24,3712]{1,0:T(8,128)(2,1)S(1)} %add_convert_fusion.4), channel_id=1, source_target_pairs={{0,56},{1,9},{4,60},{5,13},{8,0},{9,17},{12,4},{13,21},{16,8},{17,... | collective-permute-start | bytes 534536 | tf_op jit(solution)/shard_map/ppermute | solution.py:23
  178.7 9.6 %collective-permute-start.32 = (bf16[24,3712]{1,0:T(8,128)(2,1)S(1)}, bf16[24,3712]{1,0:T(8,128)(2,1)S(1)}, u32[]{:S(2)}, u32[]{:S(2)}) collective-permute-start(bf16[24,3712]{1,0:T(8,128)(2,1)S(1)} %add_convert_fusion.1), channel_id=1, source_target_pairs={{0,56},{1,9},{4,60},{5,13},{8,0},{9,17},{12,4},{13,21},{16,8},{17,... | collective-permute-start | bytes 534536 | tf_op jit(solution)/shard_map/ppermute | solution.py:23
  188.3 8.4 %collective-permute-start.33 = (bf16[24,3712]{1,0:T(8,128)(2,1)S(1)}, bf16[24,3712]{1,0:T(8,128)(2,1)S(1)}, u32[]{:S(2)}, u32[]{:S(2)}) collective-permute-start(bf16[24,3712]{1,0:T(8,128)(2,1)S(1)} %add_convert_fusion), channel_id=1, source_target_pairs={{0,60},{1,5},{4,0},{5,9},{8,4},{9,13},{12,8},{13,17},{16,12},{17,2... | collective-permute-start | bytes 534536 | tf_op jit(solution)/shard_map/ppermute | solution.py:23
  192.0 9.9 %collective-permute-start.29 = (bf16[24,3712]{1,0:T(8,128)(2,1)S(1)}, bf16[24,3712]{1,0:T(8,128)(2,1)S(1)}, u32[]{:S(2)}, u32[]{:S(2)}) collective-permute-start(bf16[24,3712]{1,0:T(8,128)(2,1)S(1)} %add_convert_fusion.3), channel_id=1, source_target_pairs={{0,56},{1,9},{4,60},{5,13},{8,0},{9,17},{12,4},{13,21},{16,8},{17,... | collective-permute-start | bytes 534536 | tf_op jit(solution)/shard_map/ppermute | solution.py:23
  202.0 3.4 %collective-permute-start.34 = (f32[12,3712]{1,0:T(8,128)S(1)}, f32[12,3712]{1,0:T(8,128)S(1)}, u32[]{:S(2)}, u32[]{:S(2)}) collective-permute-start(f32[12,3712]{1,0:T(8,128)S(1)} %slice_select_fusion), channel_id=1, source_target_pairs={{0,1},{1,0},{2,3},{3,2},{4,5},{5,4},{6,7},{7,6},{8,9},{9,8},{10,11... | collective-permute-start | bytes 534536 | tf_op jit(solution)/shard_map/ppermute | solution.py:13
  205.6 10.7 %collective-permute-start.35 = (bf16[1,12,3584]{2,1,0:T(8,128)(2,1)S(1)}, bf16[1,12,3584]{2,1,0:T(8,128)(2,1)S(1)}, u32[]{:S(2)}, u32[]{:S(2)}) collective-permute-start(bf16[1,12,3584]{2,1,0:T(8,128)(2,1)S(1)} %fusion.34), channel_id=1, source_target_pairs={{64,0},{128,64},{192,128},{256,192},{320,256},{384,320},{448,384},... | collective-permute-start | bytes 258056 | tf_op jit(solution)/shard_map/ppermute | solution.py:141

commit v2 on v1

--- a/solution.py
+++ b/solution.py
@@ -80,12 +80,15 @@
         if step == reach:
             passed_down = swap(after(far_down, lead), "c")
             passed_up[0] = swap(after(far_up[0], lead), "c")
-            passed_up[1] = swap(after(far_up[1], current[0], passed_down), "c")
+            passed_up[1] = swap(after(far_up[1], current[0]), "c")
             current = [jnp.where(first, chain, own) for chain, own in zip(current, blocks)]
         for side, chain in zip(kept, current):
             side.append(chain)
-    in_rows = jnp.concatenate(kept[0], axis=0)
-    up_rows = jnp.concatenate(kept[1], axis=0)
+    early, late = range(reach - 2), range(reach - 2, reach)
+    groups = [
+        [jnp.concatenate([side[slot] for slot in slots], axis=0) for side in kept]
+        for slots in (early, late)
+    ]
 
     def dot(left, right, left_dim, right_dim):
         return lax.dot_general(
@@ -95,7 +98,8 @@
             preferred_element_type=jnp.float32,
         )
 
-    def terms(down_part, low_part, high_part):
+    def terms(group, down_part, low_part, high_part):
+        in_rows, up_rows = groups[group]
         hid_grad = dot(up_rows, down_part, 1, 1)
         pre_act = dot(in_rows[:, :middle], low_part, 1, 0)
         pre_act = pre_act + dot(in_rows[:, middle:width], high_part, 1, 0)
@@ -104,20 +108,35 @@
         partial_dg = jnp.sum(hid_grad * (pre_act * sig_val), axis=1, keepdims=True)
         return dot(act_grad, low_part, 1, 1), dot(act_grad, high_part, 1, 1), partial_dg
 
-    found = [terms(local_down, *halves(local_up)), terms(near_down, *halves(near_up))]
-    done = (*found[0], *found[1])
-    found.append(terms(after(far_down, *done), *[after(part, *done) for part in far_up]))
-    found.append(terms(*[after(part, found[2][2]) for part in (passed_down, *passed_up)]))
-    low_dx, high_dx, token_terms = (sum(column) for column in zip(*found))
+    def weights_after(parts, *others):
+        return [after(part, *others) for part in parts]
+
+    own, near = (local_down, *halves(local_up)), (near_down, *halves(near_up))
+    found = [[terms(0, *own)], []]
+    found[1].append(terms(1, *own))
+    found[1].append(terms(1, *near))
+    found[0].append(terms(0, *near))
+    far = weights_after((far_down, *far_up), *found[1][0], *found[1][1])
+    found[1].append(terms(1, *far))
+    found[0].append(terms(0, *weights_after(far, found[1][2][2])))
+    passed = weights_after((passed_down, *passed_up), found[1][2][2])
+    found[1].append(terms(1, *passed))
+    found[0].append(terms(0, *weights_after(passed, *found[1][3])))
 
     named = ((lane % EXPERTS == expert) & (lane < 3 * EXPERTS)).astype(jnp.float32)
-    weight = jnp.sum(in_rows[:, width:].astype(jnp.float32) * named, axis=1, keepdims=True)
-    spread = sum(
-        piece * (lane == expert + at * EXPERTS).astype(jnp.float32)
-        for at, piece in enumerate(pieces(token_terms))
-    )
-    packed = jnp.concatenate([low_dx * weight, high_dx * weight, spread], axis=1)
-    parts = packed.astype(jnp.bfloat16).reshape(reach, 2 * tok, width + LANES)
+
+    def pack(group):
+        low_dx, high_dx, token_terms = (sum(column) for column in zip(*found[group]))
+        tails = groups[group][0][:, width:].astype(jnp.float32)
+        weight = jnp.sum(tails * named, axis=1, keepdims=True)
+        spread = sum(
+            piece * (lane == expert + at * EXPERTS).astype(jnp.float32)
+            for at, piece in enumerate(pieces(token_terms))
+        )
+        packed = jnp.concatenate([low_dx * weight, high_dx * weight, spread], axis=1)
+        return list(packed.astype(jnp.bfloat16).reshape(-1, 2 * tok, width + LANES))
+
+    parts = pack(0) + pack(1)
 
     def plus(moved, more):
         return moved.astype(jnp.float32) + more.astype(jnp.float32)
@@ -125,8 +144,9 @@
     even, odd = parts[reach - 1], parts[reach - 2]
     for at in range(reach - 3, 0, -2):
         cores = (0, 1) if at < reach - 3 else (0,)
-        even = plus(along(even, -2, cores), parts[at]).astype(jnp.bfloat16)
-        odd = plus(along(odd, -2), after(parts[at - 1], even)).astype(jnp.bfloat16)
+        moved = along(even, -2, cores), along(odd, -2)
+        even = plus(moved[0], parts[at]).astype(jnp.bfloat16)
+        odd = plus(moved[1], after(parts[at - 1], even)).astype(jnp.bfloat16)
     own = jnp.where(first, 0.0, parts[reach - 1].astype(jnp.float32))
     even = along(even, -2)
     odd = along(odd, -1)

time: 218 us -> 195 us (0.89)
  waiting for transfers between devices: 96.5 us -> 64.3 us
  matrix products: 11.6 us -> 21.3 us
    ppermute x24, waiting for transfers between devices: 87.8 us -> 55.6 us  [along(): return lax.ppermute(block, ('z', 'c'), route)]
    dot_general x20 -> x40, matrix products: 11.6 us -> 21.3 us  [dot(): lax.dot_general(left, right, (((left_dim,), (right_dim,)), ((), ())), pre...]
    ppermute x24, starting transfers between devices: 71.4 us -> 69.2 us  [along(): return lax.ppermute(block, ('z', 'c'), route)]
  transfers between devices with their start and end apart: 36 -> 36, of which waited for: 20 -> 19; matrix products, arithmetic and copies ran while one was open for 5% -> 12% of each run, Pallas kernels for 0% -> 0%
where the time goes in v2:
time: 195 us; the launch traced here: 193 us
  starting transfers between devices  97.7 us (50%)
  waiting for transfers between devices  64.3 us (33%)
  matrix products  21.3 us (11%)
  other arithmetic  4.5 us (2%)
  local copies, waits for them, and re-layouts  3.26 us (2%)
    ppermute x24, starting transfers between devices, along(): return lax.ppermute(block, ('z', 'c'), route)  69.2 us
    ppermute x24, waiting for transfers between devices, along(): return lax.ppermute(block, ('z', 'c'), route)  55.6 us
    ppermute x11, starting transfers between devices, swap(): return lax.ppermute(block, axis, [(0, 1), (1, 0)])  25.9 us
    dot_general x40, matrix products, dot(): lax.dot_general(left, right, (((left_dim,), (right_dim,)), ((), ())), pre...  21.3 us
    ppermute x1, waiting for transfers between devices, section(): lax.ppermute(grad_bf[None], 'pipe', [(i, i - 1) for i in range(1, section...  7.2 us
  transfers between devices with their start and end apart: 36, of which 19 were waited for; matrix products, arithmetic and copies ran while one was open for 12% of the time, Pallas kernels for 0%

profile of v2, /device:TPU:24, one launch (start us, length us, event | category | flops | bytes accessed | tf_op | source)
XLA Modules:
  0.0 192.5 jit_solution(4236455927763596272)
XLA Ops:
  0.6 2.1 %collective-permute-start = (bf16[12,3584]{1,0:T(8,128)(2,1)}, bf16[12,3584]{1,0:T(8,128)(2,1)S(1)}, u32[]{:S(2)}, u32[]{:S(2)}) collective-permute-start(bf16[12,3584]{1,0:T(8,128)(2,1)} %bitcast.98), channel_id=1, source_target_pairs={{0,1},{1,0},{2,3},{3,2},{4,5},{5,4},{6,7},{7,6},{8,9},{9,8},{10,11... | collective-permute-start | bytes 258056 | tf_op jit(solution)/shard_map/ppermute | solution.py:13
  5.4 2.4 %collective-permute-start.9 = (bf16[12,3712]{1,0:T(8,128)(2,1)S(1)}, bf16[12,3712]{1,0:T(8,128)(2,1)S(1)}, u32[]{:S(2)}, u32[]{:S(2)}) collective-permute-start(bf16[12,3712]{1,0:T(8,128)(2,1)S(1)} %pad_maximum_fusion.5), channel_id=1, source_target_pairs={{0,1},{1,0},{2,3},{3,2},{4,5},{5,4},{6,7},{7,6},{8,9},{9,8},{10,11... | collective-permute-start | bytes 267272 | tf_op jit(solution)/shard_map/ppermute | solution.py:13
  7.8 3.4 %collective-permute-start.20 = (bf16[256,3584]{1,0:T(8,128)(2,1)}, bf16[256,3584]{1,0:T(8,128)(2,1)}, u32[]{:S(2)}, u32[]{:S(2)}) collective-permute-start(bf16[256,3584]{1,0:T(8,128)(2,1)} %bitcast.94), channel_id=1, source_target_pairs={{0,2},{2,0},{1,3},{3,1},{4,6},{6,4},{5,7},{7,5},{8,10},{10,8},{9,1... | collective-permute-start | bytes 5505032 | tf_op jit(solution)/shard_map/ppermute | solution.py:13
  12.2 3.8 %collective-permute-start.1 = (bf16[24,3584]{1,0:T(8,128)(2,1)S(1)}, bf16[24,3584]{1,0:T(8,128)(2,1)S(1)}, u32[]{:S(2)}, u32[]{:S(2)}) collective-permute-start(bf16[24,3584]{1,0:T(8,128)(2,1)S(1)} %pad_maximum_fusion.4), channel_id=1, source_target_pairs={{0,4},{1,61},{4,8},{5,1},{8,12},{9,5},{12,16},{13,9},{16,20},{17,1... | collective-permute-start | bytes 516104 | tf_op jit(solution)/shard_map/ppermute | solution.py:23
  17.1 3.8 %collective-permute-start.10 = (bf16[24,3712]{1,0:T(8,128)(2,1)S(1)}, bf16[24,3712]{1,0:T(8,128)(2,1)S(1)}, u32[]{:S(2)}, u32[]{:S(2)}) collective-permute-start(bf16[24,3712]{1,0:T(8,128)(2,1)S(1)} %pad_maximum_fusion.3), channel_id=1, source_target_pairs={{0,4},{1,61},{4,8},{5,1},{8,12},{9,5},{12,16},{13,9},{16,20},{17,1... | collective-permute-start | bytes 534536 | tf_op jit(solution)/shard_map/ppermute | solution.py:23
  20.9 6.1 %collective-permute-done.1 = bf16[24,3584]{1,0:T(8,128)(2,1)S(1)} collective-permute-done((bf16[24,3584]{1,0:T(8,128)(2,1)S(1)}, bf16[24,3584]{1,0:T(8,128)(2,1)S(1)}, u32[]{:S(2)}, u32[]{:S(2)}) %collective-permute-start.1) | collective-permute-done | bytes 172064 | tf_op jit(solution)/shard_map/ppermute | solution.py:23
  27.0 1.9 collective-permute-start.2
  30.1 2.4 %collective-permute-start.21 = (bf16[1792,256]{1,0:T(8,128)(2,1)S(1)}, bf16[1792,256]{1,0:T(8,128)(2,1)S(1)}, u32[]{:S(2)}, u32[]{:S(2)}) collective-permute-start(bf16[1792,256]{1,0:T(8,128)(2,1)S(1)} %slice.91), channel_id=1, source_target_pairs={{0,2},{2,0},{1,3},{3,1},{4,6},{6,4},{5,7},{7,5},{8,10},{10,8},{9,1... | collective-permute-start | bytes 2752520 | tf_op jit(solution)/shard_map/ppermute | solution.py:13
  32.5 1.9 collective-permute-start.11
  35.5 1.9 collective-permute-start.3
  37.4 3.7 %collective-permute-done.11 = bf16[24,3712]{1,0:T(8,128)(2,1)S(1)} collective-permute-done((bf16[24,3712]{1,0:T(8,128)(2,1)S(1)}, bf16[24,3712]{1,0:T(8,128)(2,1)S(1)}, u32[]{:S(2)}, u32[]{:S(2)}) %collective-permute-start.11) | collective-permute-done | bytes 178208 | tf_op jit(solution)/shard_map/ppermute | solution.py:23
  41.2 3.4 %collective-permute-start.22 = (bf16[1792,256]{1,0:T(8,128)(2,1)S(1)}, bf16[1792,256]{1,0:T(8,128)(2,1)S(1)}, u32[]{:S(2)}, u32[]{:S(2)}) collective-permute-start(bf16[1792,256]{1,0:T(8,128)(2,1)S(1)} %slice.92), channel_id=1, source_target_pairs={{0,2},{2,0},{1,3},{3,1},{4,6},{6,4},{5,7},{7,5},{8,10},{10,8},{9,1... | collective-permute-start | bytes 2752520 | tf_op jit(solution)/shard_map/ppermute | solution.py:13
  44.6 1.9 collective-permute-start.12
  46.5 1.9 collective-permute-start.4
  48.5 4.7 %collective-permute-done.12 = bf16[24,3712]{1,0:T(8,128)(2,1)S(1)} collective-permute-done((bf16[24,3712]{1,0:T(8,128)(2,1)S(1)}, bf16[24,3712]{1,0:T(8,128)(2,1)S(1)}, u32[]{:S(2)}, u32[]{:S(2)}) %collective-permute-start.12) | collective-permute-done | bytes 178208 | tf_op jit(solution)/shard_map/ppermute | solution.py:23
  53.2 1.9 collective-permute-start.13
  55.1 1.9 collective-permute-start.5
  57.1 4.7 %collective-permute-done.13 = bf16[24,3712]{1,0:T(8,128)(2,1)S(1)} collective-permute-done((bf16[24,3712]{1,0:T(8,128)(2,1)S(1)}, bf16[24,3712]{1,0:T(8,128)(2,1)S(1)}, u32[]{:S(2)}, u32[]{:S(2)}) %collective-permute-start.13) | collective-permute-done | bytes 178208 | tf_op jit(solution)/shard_map/ppermute | solution.py:23
  61.8 1.9 collective-permute-start.14
  63.7 1.9 collective-permute-start.6
  65.7 4.7 %collective-permute-done.14 = bf16[24,3712]{1,0:T(8,128)(2,1)S(1)} collective-permute-done((bf16[24,3712]{1,0:T(8,128)(2,1)S(1)}, bf16[24,3712]{1,0:T(8,128)(2,1)S(1)}, u32[]{:S(2)}, u32[]{:S(2)}) %collective-permute-start.14) | collective-permute-done | bytes 178208 | tf_op jit(solution)/shard_map/ppermute | solution.py:23
  72.3 1.9 collective-permute-start.7
  74.2 4.7 %collective-permute-done.15 = bf16[24,3712]{1,0:T(8,128)(2,1)S(1)} collective-permute-done((bf16[24,3712]{1,0:T(8,128)(2,1)S(1)}, bf16[24,3712]{1,0:T(8,128)(2,1)S(1)}, u32[]{:S(2)}, u32[]{:S(2)}) %collective-permute-start.15) | collective-permute-done | bytes 178208 | tf_op jit(solution)/shard_map/ppermute | solution.py:23
  79.6 1.9 collective-permute-start.16
  82.8 1.9 collective-permute-start.8
  85.4 1.9 collective-permute-start.18
  91.3 1.9 collective-permute-start.17
  93.4 1.9 collective-permute-start.24
  95.3 4.6 %collective-permute-done.17 = bf16[24,3712]{1,0:T(8,128)(2,1)S(1)} collective-permute-done((bf16[24,3712]{1,0:T(8,128)(2,1)S(1)}, bf16[24,3712]{1,0:T(8,128)(2,1)S(1)}, u32[]{:S(2)}, u32[]{:S(2)}) %collective-permute-start.17) | collective-permute-done | bytes 178208 | tf_op jit(solution)/shard_map/ppermute | solution.py:23
  104.2 2.6 %collective-permute-start.23 = (bf16[256,3584]{1,0:T(8,128)(2,1)}, bf16[256,3584]{1,0:T(8,128)(2,1)S(1)}, u32[]{:S(2)}, u32[]{:S(2)}) collective-permute-start(bf16[256,3584]{1,0:T(8,128)(2,1)} %collective-permute-done.20), channel_id=1, source_target_pairs={{0,1},{1,0},{2,3},{3,2},{4,5},{5,4},{6,7},{7,6},{8,9},{9,8},{10,11... | collective-permute-start | bytes 5505032 | tf_op jit(solution)/shard_map/ppermute | solution.py:13
  109.6 2.3 %multiply_convert_fusion.5 = (bf16[48,256]{1,0:T(8,128)(2,1)S(1)}, f32[48]{0:T(128)S(1)}) fusion(f32[48,256]{1,0:T(8,128)S(1)} %convolution_add_fusion.13, bf16[256,3584]{1,0:T(8,128)(2,1)} %collective-permute-done.20, bf16[24,3584]{1,0:T(8,128)(2,1)S(1)} %broadcast_select_fusion.1, bf16[24,3584]{1,0:T(8,128)(2,1)S(1)} %collective-permute-done.7), kind=kOutput, calls=%fused_computation.118 | convolution fusion | flops 88915920 | bytes 2252992 | tf_op jit(solution)/shard_map/dot_general | solution.py:94
  115.1 2.3 %multiply_convert_fusion.1 = (bf16[144,256]{1,0:T(8,128)(2,1)S(1)}, f32[144]{0:T(256)S(1)}) fusion(f32[144,256]{1,0:T(8,128)S(1)} %convolution_add_fusion.9, bf16[144,3584]{1,0:T(8,128)(2,1)S(1)} %constant_dynamic-update-slice_fusion, bf16[256,3584]{1,0:T(8,128)(2,1)} %collective-permute-done.20), kind=kOutput, calls=%fused_computation.99 | convolution fusion | flops 264683376 | bytes 3088960 | tf_op jit(solution)/shard_map/dot_general | solution.py:94
  124.0 5.0 %collective-permute-start.30 = (bf16[24,3712]{1,0:T(8,128)(2,1)S(1)}, bf16[24,3712]{1,0:T(8,128)(2,1)S(1)}, u32[]{:S(2)}, u32[]{:S(2)}) collective-permute-start(bf16[24,3712]{1,0:T(8,128)(2,1)S(1)} %get-tuple-element.53), channel_id=1, source_target_pairs={{0,56},{1,9},{4,60},{5,13},{8,0},{9,17},{12,4},{13,21},{16,8},{17,... | collective-permute-start | bytes 534536 | tf_op jit(solution)/shard_map/ppermute | solution.py:23
  129.0 4.9 %collective-permute-start.26 = (bf16[24,3712]{1,0:T(8,128)(2,1)S(1)}, bf16[24,3712]{1,0:T(8,128)(2,1)S(1)}, u32[]{:S(2)}, u32[]{:S(2)}) collective-permute-start(bf16[24,3712]{1,0:T(8,128)(2,1)S(1)} %get-tuple-element.54), channel_id=1, source_target_pairs={{0,56},{4,60},{8,0},{12,4},{16,8},{20,12},{24,16},{28,20},{32,24},... | collective-permute-start | bytes 534536 | tf_op jit(solution)/shard_map/ppermute | solution.py:23
  134.2 4.2 %collective-permute-done.26 = bf16[24,3712]{1,0:T(8,128)(2,1)S(1)} collective-permute-done((bf16[24,3712]{1,0:T(8,128)(2,1)S(1)}, bf16[24,3712]{1,0:T(8,128)(2,1)S(1)}, u32[]{:S(2)}, u32[]{:S(2)}) %collective-permute-start.26) | collective-permute-done | bytes 178208 | tf_op jit(solution)/shard_map/ppermute | solution.py:23
  138.4 6.3 %collective-permute-start.27 = (bf16[24,3712]{1,0:T(8,128)(2,1)S(1)}, bf16[24,3712]{1,0:T(8,128)(2,1)S(1)}, u32[]{:S(2)}, u32[]{:S(2)}) collective-permute-start(bf16[24,3712]{1,0:T(8,128)(2,1)S(1)} %add_convert_fusion.5), channel_id=1, source_target_pairs={{0,56},{1,9},{4,60},{5,13},{8,0},{9,17},{12,4},{13,21},{16,8},{17,... | collective-permute-start | bytes 534536 | tf_op jit(solution)/shard_map/ppermute | solution.py:23
  144.8 3.0 %collective-permute-start.31 = (bf16[24,3712]{1,0:T(8,128)(2,1)S(1)}, bf16[24,3712]{1,0:T(8,128)(2,1)S(1)}, u32[]{:S(2)}, u32[]{:S(2)}) collective-permute-start(bf16[24,3712]{1,0:T(8,128)(2,1)S(1)} %add_convert_fusion.2), channel_id=1, source_target_pairs={{0,56},{1,9},{4,60},{5,13},{8,0},{9,17},{12,4},{13,21},{16,8},{17,... | collective-permute-start | bytes 534536 | tf_op jit(solution)/shard_map/ppermute | solution.py:23
  147.8 3.6 %collective-permute-done.27 = bf16[24,3712]{1,0:T(8,128)(2,1)S(1)} collective-permute-done((bf16[24,3712]{1,0:T(8,128)(2,1)S(1)}, bf16[24,3712]{1,0:T(8,128)(2,1)S(1)}, u32[]{:S(2)}, u32[]{:S(2)}) %collective-permute-start.27) | collective-permute-done | bytes 178208 | tf_op jit(solution)/shard_map/ppermute | solution.py:23
  151.5 6.5 %collective-permute-start.28 = (bf16[24,3712]{1,0:T(8,128)(2,1)S(1)}, bf16[24,3712]{1,0:T(8,128)(2,1)S(1)}, u32[]{:S(2)}, u32[]{:S(2)}) collective-permute-start(bf16[24,3712]{1,0:T(8,128)(2,1)S(1)} %add_convert_fusion.4), channel_id=1, source_target_pairs={{0,56},{1,9},{4,60},{5,13},{8,0},{9,17},{12,4},{13,21},{16,8},{17,... | collective-permute-start | bytes 534536 | tf_op jit(solution)/shard_map/ppermute | solution.py:23
  158.0 1.9 %collective-permute-start.32 = (bf16[24,3712]{1,0:T(8,128)(2,1)S(1)}, bf16[24,3712]{1,0:T(8,128)(2,1)S(1)}, u32[]{:S(2)}, u32[]{:S(2)}) collective-permute-start(bf16[24,3712]{1,0:T(8,128)(2,1)S(1)} %add_convert_fusion.1), channel_id=1, source_target_pairs={{0,56},{1,9},{4,60},{5,13},{8,0},{9,17},{12,4},{13,21},{16,8},{17,... | collective-permute-start | bytes 534536 | tf_op jit(solution)/shard_map/ppermute | solution.py:23
  160.0 3.0 %collective-permute-done.28 = bf16[24,3712]{1,0:T(8,128)(2,1)S(1)} collective-permute-done((bf16[24,3712]{1,0:T(8,128)(2,1)S(1)}, bf16[24,3712]{1,0:T(8,128)(2,1)S(1)}, u32[]{:S(2)}, u32[]{:S(2)}) %collective-permute-start.28) | collective-permute-done | bytes 178208 | tf_op jit(solution)/shard_map/ppermute | solution.py:23
  163.0 3.3 %collective-permute-done.32 = bf16[24,3712]{1,0:T(8,128)(2,1)S(1)} collective-permute-done((bf16[24,3712]{1,0:T(8,128)(2,1)S(1)}, bf16[24,3712]{1,0:T(8,128)(2,1)S(1)}, u32[]{:S(2)}, u32[]{:S(2)}) %collective-permute-start.32) | collective-permute-done | bytes 178208 | tf_op jit(solution)/shard_map/ppermute | solution.py:23
  166.3 1.9 collective-permute-start.33
  168.3 5.1 %collective-permute-start.29 = (bf16[24,3712]{1,0:T(8,128)(2,1)S(1)}, bf16[24,3712]{1,0:T(8,128)(2,1)S(1)}, u32[]{:S(2)}, u32[]{:S(2)}) collective-permute-start(bf16[24,3712]{1,0:T(8,128)(2,1)S(1)} %add_convert_fusion.3), channel_id=1, source_target_pairs={{0,56},{1,9},{4,60},{5,13},{8,0},{9,17},{12,4},{13,21},{16,8},{17,... | collective-permute-start | bytes 534536 | tf_op jit(solution)/shard_map/ppermute | solution.py:23
  173.7 3.8 %collective-permute-done.29 = bf16[24,3712]{1,0:T(8,128)(2,1)S(1)} collective-permute-done((bf16[24,3712]{1,0:T(8,128)(2,1)S(1)}, bf16[24,3712]{1,0:T(8,128)(2,1)S(1)}, u32[]{:S(2)}, u32[]{:S(2)}) %collective-permute-start.29) | collective-permute-done | bytes 178208 | tf_op jit(solution)/shard_map/ppermute | solution.py:23
  177.7 1.9 collective-permute-start.34
  181.2 2.7 %collective-permute-start.35 = (bf16[1,12,3584]{2,1,0:T(8,128)(2,1)S(1)}, bf16[1,12,3584]{2,1,0:T(8,128)(2,1)S(1)}, u32[]{:S(2)}, u32[]{:S(2)}) collective-permute-start(bf16[1,12,3584]{2,1,0:T(8,128)(2,1)S(1)} %fusion.56), channel_id=1, source_target_pairs={{64,0},{128,64},{192,128},{256,192},{320,256},{384,320},{448,384},... | collective-permute-start | bytes 258056 | tf_op jit(solution)/shard_map/ppermute | solution.py:161
  184.7 7.2 %collective-permute-done.35 = bf16[1,12,3584]{2,1,0:T(8,128)(2,1)S(1)} collective-permute-done((bf16[1,12,3584]{2,1,0:T(8,128)(2,1)S(1)}, bf16[1,12,3584]{2,1,0:T(8,128)(2,1)S(1)}, u32[]{:S(2)}, u32[]{:S(2)}) %collective-permute-start.35) | collective-permute-done | bytes 86048 | tf_op jit(solution)/shard_map/ppermute | solution.py:161
  (124 shorter events, 36.3 us)
Async XLA Ops:
  0.6 29.4 %copy-start = (bf16[1,3584,256]{2,1,0:T(8,128)(2,1)S(1)}, bf16[1,3584,256]{2,1,0:T(8,128)(2,1)}, u32[]{:S(2)}) copy-start(bf16[1,3584,256]{2,1,0:T(8,128)(2,1)} %param.10) | copy-start | bytes 5505028
  0.6 10.6 %collective-permute-start = (bf16[12,3584]{1,0:T(8,128)(2,1)}, bf16[12,3584]{1,0:T(8,128)(2,1)S(1)}, u32[]{:S(2)}, u32[]{:S(2)}) collective-permute-start(bf16[12,3584]{1,0:T(8,128)(2,1)} %bitcast.98), channel_id=1, source_target_pairs={{0,1},{1,0},{2,3},{3,2},{4,5},{5,4},{6,7},{7,6},{8,9},{9,8},{10,11... | collective-permute-start | bytes 258056 | tf_op jit(solution)/shard_map/ppermute | solution.py:13
  5.4 10.7 %collective-permute-start.9 = (bf16[12,3712]{1,0:T(8,128)(2,1)S(1)}, bf16[12,3712]{1,0:T(8,128)(2,1)S(1)}, u32[]{:S(2)}, u32[]{:S(2)}) collective-permute-start(bf16[12,3712]{1,0:T(8,128)(2,1)S(1)} %pad_maximum_fusion.5), channel_id=1, source_target_pairs={{0,1},{1,0},{2,3},{3,2},{4,5},{5,4},{6,7},{7,6},{8,9},{9,8},{10,11... | collective-permute-start | bytes 267272 | tf_op jit(solution)/shard_map/ppermute | solution.py:13
  7.8 96.5 %collective-permute-start.20 = (bf16[256,3584]{1,0:T(8,128)(2,1)}, bf16[256,3584]{1,0:T(8,128)(2,1)}, u32[]{:S(2)}, u32[]{:S(2)}) collective-permute-start(bf16[256,3584]{1,0:T(8,128)(2,1)} %bitcast.94), channel_id=1, source_target_pairs={{0,2},{2,0},{1,3},{3,1},{4,6},{6,4},{5,7},{7,5},{8,10},{10,8},{9,1... | collective-permute-start | bytes 5505032 | tf_op jit(solution)/shard_map/ppermute | solution.py:13
  12.2 14.8 %collective-permute-start.1 = (bf16[24,3584]{1,0:T(8,128)(2,1)S(1)}, bf16[24,3584]{1,0:T(8,128)(2,1)S(1)}, u32[]{:S(2)}, u32[]{:S(2)}) collective-permute-start(bf16[24,3584]{1,0:T(8,128)(2,1)S(1)} %pad_maximum_fusion.4), channel_id=1, source_target_pairs={{0,4},{1,61},{4,8},{5,1},{8,12},{9,5},{12,16},{13,9},{16,20},{17,1... | collective-permute-start | bytes 516104 | tf_op jit(solution)/shard_map/ppermute | solution.py:23
  17.1 12.9 %collective-permute-start.10 = (bf16[24,3712]{1,0:T(8,128)(2,1)S(1)}, bf16[24,3712]{1,0:T(8,128)(2,1)S(1)}, u32[]{:S(2)}, u32[]{:S(2)}) collective-permute-start(bf16[24,3712]{1,0:T(8,128)(2,1)S(1)} %pad_maximum_fusion.3), channel_id=1, source_target_pairs={{0,4},{1,61},{4,8},{5,1},{8,12},{9,5},{12,16},{13,9},{16,20},{17,1... | collective-permute-start | bytes 534536 | tf_op jit(solution)/shard_map/ppermute | solution.py:23
  27.0 8.5 %collective-permute-start.2 = (bf16[24,3584]{1,0:T(8,128)(2,1)S(1)}, bf16[24,3584]{1,0:T(8,128)(2,1)S(1)}, u32[]{:S(2)}, u32[]{:S(2)}) collective-permute-start(bf16[24,3584]{1,0:T(8,128)(2,1)S(1)} %collective-permute-done.1), channel_id=1, source_target_pairs={{0,4},{1,61},{4,8},{5,1},{8,12},{9,5},{12,16},{13,9},{16,20},{17,1... | collective-permute-start | bytes 516104 | tf_op jit(solution)/shard_map/ppermute | solution.py:23
  30.1 55.3 %collective-permute-start.21 = (bf16[1792,256]{1,0:T(8,128)(2,1)S(1)}, bf16[1792,256]{1,0:T(8,128)(2,1)S(1)}, u32[]{:S(2)}, u32[]{:S(2)}) collective-permute-start(bf16[1792,256]{1,0:T(8,128)(2,1)S(1)} %slice.91), channel_id=1, source_target_pairs={{0,2},{2,0},{1,3},{3,1},{4,6},{6,4},{5,7},{7,5},{8,10},{10,8},{9,1... | collective-permute-start | bytes 2752520 | tf_op jit(solution)/shard_map/ppermute | solution.py:13
  32.5 8.6 %collective-permute-start.11 = (bf16[24,3712]{1,0:T(8,128)(2,1)S(1)}, bf16[24,3712]{1,0:T(8,128)(2,1)S(1)}, u32[]{:S(2)}, u32[]{:S(2)}) collective-permute-start(bf16[24,3712]{1,0:T(8,128)(2,1)S(1)} %collective-permute-done.10), channel_id=1, source_target_pairs={{0,4},{1,61},{4,8},{5,1},{8,12},{9,5},{12,16},{13,9},{16,20},{17,1... | collective-permute-start | bytes 534536 | tf_op jit(solution)/shard_map/ppermute | solution.py:23
  35.5 11.0 %collective-permute-start.3 = (bf16[24,3584]{1,0:T(8,128)(2,1)S(1)}, bf16[24,3584]{1,0:T(8,128)(2,1)S(1)}, u32[]{:S(2)}, u32[]{:S(2)}) collective-permute-start(bf16[24,3584]{1,0:T(8,128)(2,1)S(1)} %collective-permute-done.2), channel_id=1, source_target_pairs={{0,4},{1,61},{4,8},{5,1},{8,12},{9,5},{12,16},{13,9},{16,20},{17,1... | collective-permute-start | bytes 516104 | tf_op jit(solution)/shard_map/ppermute | solution.py:23
  41.2 52.2 %collective-permute-start.22 = (bf16[1792,256]{1,0:T(8,128)(2,1)S(1)}, bf16[1792,256]{1,0:T(8,128)(2,1)S(1)}, u32[]{:S(2)}, u32[]{:S(2)}) collective-permute-start(bf16[1792,256]{1,0:T(8,128)(2,1)S(1)} %slice.92), channel_id=1, source_target_pairs={{0,2},{2,0},{1,3},{3,1},{4,6},{6,4},{5,7},{7,5},{8,10},{10,8},{9,1... | collective-permute-start | bytes 2752520 | tf_op jit(solution)/shard_map/ppermute | solution.py:13
  44.6 8.6 %collective-permute-start.12 = (bf16[24,3712]{1,0:T(8,128)(2,1)S(1)}, bf16[24,3712]{1,0:T(8,128)(2,1)S(1)}, u32[]{:S(2)}, u32[]{:S(2)}) collective-permute-start(bf16[24,3712]{1,0:T(8,128)(2,1)S(1)} %collective-permute-done.11), channel_id=1, source_target_pairs={{0,4},{1,61},{4,8},{5,1},{8,12},{9,5},{12,16},{13,9},{16,20},{17,1... | collective-permute-start | bytes 534536 | tf_op jit(solution)/shard_map/ppermute | solution.py:23
  46.5 8.6 %collective-permute-start.4 = (bf16[24,3584]{1,0:T(8,128)(2,1)S(1)}, bf16[24,3584]{1,0:T(8,128)(2,1)S(1)}, u32[]{:S(2)}, u32[]{:S(2)}) collective-permute-start(bf16[24,3584]{1,0:T(8,128)(2,1)S(1)} %collective-permute-done.3), channel_id=1, source_target_pairs={{0,4},{1,61},{4,8},{5,1},{8,12},{9,5},{12,16},{13,9},{16,20},{17,1... | collective-permute-start | bytes 516104 | tf_op jit(solution)/shard_map/ppermute | solution.py:23
  53.2 8.6 %collective-permute-start.13 = (bf16[24,3712]{1,0:T(8,128)(2,1)S(1)}, bf16[24,3712]{1,0:T(8,128)(2,1)S(1)}, u32[]{:S(2)}, u32[]{:S(2)}) collective-permute-start(bf16[24,3712]{1,0:T(8,128)(2,1)S(1)} %collective-permute-done.12), channel_id=1, source_target_pairs={{0,4},{1,61},{4,8},{5,1},{8,12},{9,5},{12,16},{13,9},{16,20},{17,1... | collective-permute-start | bytes 534536 | tf_op jit(solution)/shard_map/ppermute | solution.py:23
  55.1 8.6 %collective-permute-start.5 = (bf16[24,3584]{1,0:T(8,128)(2,1)S(1)}, bf16[24,3584]{1,0:T(8,128)(2,1)S(1)}, u32[]{:S(2)}, u32[]{:S(2)}) collective-permute-start(bf16[24,3584]{1,0:T(8,128)(2,1)S(1)} %collective-permute-done.4), channel_id=1, source_target_pairs={{0,4},{1,61},{4,8},{5,1},{8,12},{9,5},{12,16},{13,9},{16,20},{17,1... | collective-permute-start | bytes 516104 | tf_op jit(solution)/shard_map/ppermute | solution.py:23
  61.8 8.6 %collective-permute-start.14 = (bf16[24,3712]{1,0:T(8,128)(2,1)S(1)}, bf16[24,3712]{1,0:T(8,128)(2,1)S(1)}, u32[]{:S(2)}, u32[]{:S(2)}) collective-permute-start(bf16[24,3712]{1,0:T(8,128)(2,1)S(1)} %collective-permute-done.13), channel_id=1, source_target_pairs={{0,4},{1,61},{4,8},{5,1},{8,12},{9,5},{12,16},{13,9},{16,20},{17,1... | collective-permute-start | bytes 534536 | tf_op jit(solution)/shard_map/ppermute | solution.py:23
  63.7 8.6 %collective-permute-start.6 = (bf16[24,3584]{1,0:T(8,128)(2,1)S(1)}, bf16[24,3584]{1,0:T(8,128)(2,1)S(1)}, u32[]{:S(2)}, u32[]{:S(2)}) collective-permute-start(bf16[24,3584]{1,0:T(8,128)(2,1)S(1)} %collective-permute-done.5), channel_id=1, source_target_pairs={{0,4},{1,61},{4,8},{5,1},{8,12},{9,5},{12,16},{13,9},{16,20},{17,1... | collective-permute-start | bytes 516104 | tf_op jit(solution)/shard_map/ppermute | solution.py:23
  70.3 8.6 %collective-permute-start.15 = (bf16[24,3712]{1,0:T(8,128)(2,1)S(1)}, bf16[24,3712]{1,0:T(8,128)(2,1)S(1)}, u32[]{:S(2)}, u32[]{:S(2)}) collective-permute-start(bf16[24,3712]{1,0:T(8,128)(2,1)S(1)} %collective-permute-done.14), channel_id=1, source_target_pairs={{0,4},{1,61},{4,8},{5,1},{8,12},{9,5},{12,16},{13,9},{16,20},{17,1... | collective-permute-start | bytes 534536 | tf_op jit(solution)/shard_map/ppermute | solution.py:23
  72.3 10.6 %collective-permute-start.7 = (bf16[24,3584]{1,0:T(8,128)(2,1)S(1)}, bf16[24,3584]{1,0:T(8,128)(2,1)S(1)}, u32[]{:S(2)}, u32[]{:S(2)}) collective-permute-start(bf16[24,3584]{1,0:T(8,128)(2,1)S(1)} %collective-permute-done.6), channel_id=1, source_target_pairs={{0,4},{1,61},{4,8},{5,1},{8,12},{9,5},{12,16},{13,9},{16,20},{17,1... | collective-permute-start | bytes 516104 | tf_op jit(solution)/shard_map/ppermute | solution.py:23
  78.9 2.6 %copy-start.1 = (bf16[1,256,3584]{2,1,0:T(8,128)(2,1)S(1)}, bf16[1,256,3584]{2,1,0:T(8,128)(2,1)}, u32[]{:S(2)}) copy-start(bf16[1,256,3584]{2,1,0:T(8,128)(2,1)} %param.11) | copy-start | bytes 5505028
  79.6 8.6 %collective-permute-start.16 = (bf16[24,3712]{1,0:T(8,128)(2,1)S(1)}, bf16[24,3712]{1,0:T(8,128)(2,1)S(1)}, u32[]{:S(2)}, u32[]{:S(2)}) collective-permute-start(bf16[24,3712]{1,0:T(8,128)(2,1)S(1)} %collective-permute-done.15), channel_id=1, source_target_pairs={{0,4},{1,61},{4,8},{5,1},{8,12},{9,5},{12,16},{13,9},{16,20},{17,1... | collective-permute-start | bytes 534536 | tf_op jit(solution)/shard_map/ppermute | solution.py:23
  82.8 8.5 %collective-permute-start.8 = (bf16[24,3584]{1,0:T(8,128)(2,1)S(1)}, bf16[24,3584]{1,0:T(8,128)(2,1)S(1)}, u32[]{:S(2)}, u32[]{:S(2)}) collective-permute-start(bf16[24,3584]{1,0:T(8,128)(2,1)S(1)} %collective-permute-done.7), channel_id=1, source_target_pairs={{0,4},{4,8},{8,12},{12,16},{16,20},{20,24},{24,28},{28,32},{32,36}... | collective-permute-start | bytes 516104 | tf_op jit(solution)/shard_map/ppermute | solution.py:23
  85.4 22.1 %collective-permute-start.18 = (bf16[256,3584]{1,0:T(8,128)(2,1)S(1)}, bf16[256,3584]{1,0:T(8,128)(2,1)S(1)}, u32[]{:S(2)}, u32[]{:S(2)}) collective-permute-start(bf16[256,3584]{1,0:T(8,128)(2,1)S(1)} %bitcast.95), channel_id=1, source_target_pairs={{0,1},{1,0},{2,3},{3,2},{4,5},{5,4},{6,7},{7,6},{8,9},{9,8},{10,11... | collective-permute-start | bytes 5505032 | tf_op jit(solution)/shard_map/ppermute | solution.py:13
  88.1 18.7 %collective-permute-start.19 = (bf16[3584,256]{1,0:T(8,128)(2,1)S(1)}, bf16[3584,256]{1,0:T(8,128)(2,1)S(1)}, u32[]{:S(2)}, u32[]{:S(2)}) collective-permute-start(bf16[3584,256]{1,0:T(8,128)(2,1)S(1)} %bitcast.93), channel_id=1, source_target_pairs={{0,1},{1,0},{2,3},{3,2},{4,5},{5,4},{6,7},{7,6},{8,9},{9,8},{10,11... | collective-permute-start | bytes 5505032 | tf_op jit(solution)/shard_map/ppermute | solution.py:13
  91.3 8.6 %collective-permute-start.17 = (bf16[24,3712]{1,0:T(8,128)(2,1)S(1)}, bf16[24,3712]{1,0:T(8,128)(2,1)S(1)}, u32[]{:S(2)}, u32[]{:S(2)}) collective-permute-start(bf16[24,3712]{1,0:T(8,128)(2,1)S(1)} %collective-permute-done.16), channel_id=1, source_target_pairs={{0,4},{4,8},{8,12},{12,16},{16,20},{20,24},{24,28},{28,32},{32,36}... | collective-permute-start | bytes 534536 | tf_op jit(solution)/shard_map/ppermute | solution.py:23
  93.4 18.8 %collective-permute-start.24 = (bf16[1792,256]{1,0:T(8,128)(2,1)S(1)}, bf16[1792,256]{1,0:T(8,128)(2,1)S(1)}, u32[]{:S(2)}, u32[]{:S(2)}) collective-permute-start(bf16[1792,256]{1,0:T(8,128)(2,1)S(1)} %collective-permute-done.21), channel_id=1, source_target_pairs={{0,1},{1,0},{2,3},{3,2},{4,5},{5,4},{6,7},{7,6},{8,9},{9,8},{10,11... | collective-permute-start | bytes 2752520 | tf_op jit(solution)/shard_map/ppermute | solution.py:13
  99.9 12.0 %collective-permute-start.25 = (bf16[1792,256]{1,0:T(8,128)(2,1)S(1)}, bf16[1792,256]{1,0:T(8,128)(2,1)S(1)}, u32[]{:S(2)}, u32[]{:S(2)}) collective-permute-start(bf16[1792,256]{1,0:T(8,128)(2,1)S(1)} %collective-permute-done.22), channel_id=1, source_target_pairs={{0,1},{1,0},{2,3},{3,2},{4,5},{5,4},{6,7},{7,6},{8,9},{9,8},{10,11... | collective-permute-start | bytes 2752520 | tf_op jit(solution)/shard_map/ppermute | solution.py:13
  104.2 14.6 %collective-permute-start.23 = (bf16[256,3584]{1,0:T(8,128)(2,1)}, bf16[256,3584]{1,0:T(8,128)(2,1)S(1)}, u32[]{:S(2)}, u32[]{:S(2)}) collective-permute-start(bf16[256,3584]{1,0:T(8,128)(2,1)} %collective-permute-done.20), channel_id=1, source_target_pairs={{0,1},{1,0},{2,3},{3,2},{4,5},{5,4},{6,7},{7,6},{8,9},{9,8},{10,11... | collective-permute-start | bytes 5505032 | tf_op jit(solution)/shard_map/ppermute | solution.py:13
  124.0 20.8 %collective-permute-start.30 = (bf16[24,3712]{1,0:T(8,128)(2,1)S(1)}, bf16[24,3712]{1,0:T(8,128)(2,1)S(1)}, u32[]{:S(2)}, u32[]{:S(2)}) collective-permute-start(bf16[24,3712]{1,0:T(8,128)(2,1)S(1)} %get-tuple-element.53), channel_id=1, source_target_pairs={{0,56},{1,9},{4,60},{5,13},{8,0},{9,17},{12,4},{13,21},{16,8},{17,... | collective-permute-start | bytes 534536 | tf_op jit(solution)/shard_map/ppermute | solution.py:23
  129.0 9.4 %collective-permute-start.26 = (bf16[24,3712]{1,0:T(8,128)(2,1)S(1)}, bf16[24,3712]{1,0:T(8,128)(2,1)S(1)}, u32[]{:S(2)}, u32[]{:S(2)}) collective-permute-start(bf16[24,3712]{1,0:T(8,128)(2,1)S(1)} %get-tuple-element.54), channel_id=1, source_target_pairs={{0,56},{4,60},{8,0},{12,4},{16,8},{20,12},{24,16},{28,20},{32,24},... | collective-permute-start | bytes 534536 | tf_op jit(solution)/shard_map/ppermute | solution.py:23
  138.4 13.0 %collective-permute-start.27 = (bf16[24,3712]{1,0:T(8,128)(2,1)S(1)}, bf16[24,3712]{1,0:T(8,128)(2,1)S(1)}, u32[]{:S(2)}, u32[]{:S(2)}) collective-permute-start(bf16[24,3712]{1,0:T(8,128)(2,1)S(1)} %add_convert_fusion.5), channel_id=1, source_target_pairs={{0,56},{1,9},{4,60},{5,13},{8,0},{9,17},{12,4},{13,21},{16,8},{17,... | collective-permute-start | bytes 534536 | tf_op jit(solution)/shard_map/ppermute | solution.py:23
  144.8 13.1 %collective-permute-start.31 = (bf16[24,3712]{1,0:T(8,128)(2,1)S(1)}, bf16[24,3712]{1,0:T(8,128)(2,1)S(1)}, u32[]{:S(2)}, u32[]{:S(2)}) collective-permute-start(bf16[24,3712]{1,0:T(8,128)(2,1)S(1)} %add_convert_fusion.2), channel_id=1, source_target_pairs={{0,56},{1,9},{4,60},{5,13},{8,0},{9,17},{12,4},{13,21},{16,8},{17,... | collective-permute-start | bytes 534536 | tf_op jit(solution)/shard_map/ppermute | solution.py:23
  151.5 11.5 %collective-permute-start.28 = (bf16[24,3712]{1,0:T(8,128)(2,1)S(1)}, bf16[24,3712]{1,0:T(8,128)(2,1)S(1)}, u32[]{:S(2)}, u32[]{:S(2)}) collective-permute-start(bf16[24,3712]{1,0:T(8,128)(2,1)S(1)} %add_convert_fusion.4), channel_id=1, source_target_pairs={{0,56},{1,9},{4,60},{5,13},{8,0},{9,17},{12,4},{13,21},{16,8},{17,... | collective-permute-start | bytes 534536 | tf_op jit(solution)/shard_map/ppermute | solution.py:23
  158.0 8.3 %collective-permute-start.32 = (bf16[24,3712]{1,0:T(8,128)(2,1)S(1)}, bf16[24,3712]{1,0:T(8,128)(2,1)S(1)}, u32[]{:S(2)}, u32[]{:S(2)}) collective-permute-start(bf16[24,3712]{1,0:T(8,128)(2,1)S(1)} %add_convert_fusion.1), channel_id=1, source_target_pairs={{0,56},{1,9},{4,60},{5,13},{8,0},{9,17},{12,4},{13,21},{16,8},{17,... | collective-permute-start | bytes 534536 | tf_op jit(solution)/shard_map/ppermute | solution.py:23
  166.3 7.4 %collective-permute-start.33 = (bf16[24,3712]{1,0:T(8,128)(2,1)S(1)}, bf16[24,3712]{1,0:T(8,128)(2,1)S(1)}, u32[]{:S(2)}, u32[]{:S(2)}) collective-permute-start(bf16[24,3712]{1,0:T(8,128)(2,1)S(1)} %add_convert_fusion), channel_id=1, source_target_pairs={{0,60},{1,5},{4,0},{5,9},{8,4},{9,13},{12,8},{13,17},{16,12},{17,2... | collective-permute-start | bytes 534536 | tf_op jit(solution)/shard_map/ppermute | solution.py:23
  168.3 9.3 %collective-permute-start.29 = (bf16[24,3712]{1,0:T(8,128)(2,1)S(1)}, bf16[24,3712]{1,0:T(8,128)(2,1)S(1)}, u32[]{:S(2)}, u32[]{:S(2)}) collective-permute-start(bf16[24,3712]{1,0:T(8,128)(2,1)S(1)} %add_convert_fusion.3), channel_id=1, source_target_pairs={{0,56},{1,9},{4,60},{5,13},{8,0},{9,17},{12,4},{13,21},{16,8},{17,... | collective-permute-start | bytes 534536 | tf_op jit(solution)/shard_map/ppermute | solution.py:23
  177.7 3.4 %collective-permute-start.34 = (f32[12,3712]{1,0:T(8,128)S(1)}, f32[12,3712]{1,0:T(8,128)S(1)}, u32[]{:S(2)}, u32[]{:S(2)}) collective-permute-start(f32[12,3712]{1,0:T(8,128)S(1)} %slice_select_fusion), channel_id=1, source_target_pairs={{0,1},{1,0},{2,3},{3,2},{4,5},{5,4},{6,7},{7,6},{8,9},{9,8},{10,11... | collective-permute-start | bytes 534536 | tf_op jit(solution)/shard_map/ppermute | solution.py:13
  181.2 10.7 %collective-permute-start.35 = (bf16[1,12,3584]{2,1,0:T(8,128)(2,1)S(1)}, bf16[1,12,3584]{2,1,0:T(8,128)(2,1)S(1)}, u32[]{:S(2)}, u32[]{:S(2)}) collective-permute-start(bf16[1,12,3584]{2,1,0:T(8,128)(2,1)S(1)} %fusion.56), channel_id=1, source_target_pairs={{64,0},{128,64},{192,128},{256,192},{320,256},{384,320},{448,384},... | collective-permute-start | bytes 258056 | tf_op jit(solution)/shard_map/ppermute | solution.py:161

commit v3 on v1

--- a/solution.py
+++ b/solution.py
@@ -60,7 +60,6 @@
     blocks = [packed_in, packed_out]
 
     halves = lambda whole: (whole[:middle], whole[middle:])
-    far_up, passed_up = [None, None], [None, None]
     far_down = swap(local_down, "xl")
 
     current, kept = list(blocks), [[], []]
@@ -70,17 +69,14 @@
             current[side] = along(current[side], 1, cores)
         lead = kept[0][-1] if step > 1 else blocks[0]
         if step == 2:
-            far_up[0] = swap(after(local_up, lead)[:middle], "xl")
-        if step == 3:
-            far_up[1] = swap(after(local_up, lead)[middle:], "xl")
+            far_up = swap(after(local_up, lead), "xl")
         if step == 4:
             near_down = swap(after(local_down, lead), "c")
-        if step == 5:
+        if step == 6:
             near_up = swap(after(local_up, lead), "c")
         if step == reach:
             passed_down = swap(after(far_down, lead), "c")
-            passed_up[0] = swap(after(far_up[0], lead), "c")
-            passed_up[1] = swap(after(far_up[1], current[0], passed_down), "c")
+            passed_up = swap(after(far_up, current[0]), "c")
             current = [jnp.where(first, chain, own) for chain, own in zip(current, blocks)]
         for side, chain in zip(kept, current):
             side.append(chain)
@@ -104,10 +100,12 @@
         partial_dg = jnp.sum(hid_grad * (pre_act * sig_val), axis=1, keepdims=True)
         return dot(act_grad, low_part, 1, 1), dot(act_grad, high_part, 1, 1), partial_dg
 
-    found = [terms(local_down, *halves(local_up)), terms(near_down, *halves(near_up))]
+    found = [terms(local_down, *halves(local_up))]
+    found.append(terms(near_down, *halves(near_up)))
     done = (*found[0], *found[1])
-    found.append(terms(after(far_down, *done), *[after(part, *done) for part in far_up]))
-    found.append(terms(*[after(part, found[2][2]) for part in (passed_down, *passed_up)]))
+    found.append(terms(after(far_down, *done), *halves(after(far_up, *done))))
+    last = found[2][2]
+    found.append(terms(after(passed_down, last), *halves(after(passed_up, last))))
     low_dx, high_dx, token_terms = (sum(column) for column in zip(*found))
 
     named = ((lane % EXPERTS == expert) & (lane < 3 * EXPERTS)).astype(jnp.float32)

time: 218 us -> 195 us (0.89)
  waiting for transfers between devices: 96.5 us -> 78.3 us
  starting transfers between devices: 99.6 us -> 94.8 us
    ppermute x24, waiting for transfers between devices: 87.8 us -> 69.6 us  [along(): return lax.ppermute(block, ('z', 'c'), route)]
    ppermute x11 -> x9, starting transfers between devices: 25.6 us -> 20.2 us  [swap(): return lax.ppermute(block, axis, [(0, 1), (1, 0)])]
  transfers between devices with their start and end apart: 36 -> 34, of which waited for: 20 -> 18; matrix products, arithmetic and copies ran while one was open for 5% -> 7% of each run, Pallas kernels for 0% -> 0%
where the time goes in v3:
time: 195 us; the launch traced here: 194 us
  starting transfers between devices  94.8 us (49%)
  waiting for transfers between devices  78.3 us (40%)
  matrix products  11.6 us (6%)
  other arithmetic  4.29 us (2%)
  local copies, waits for them, and re-layouts  3.31 us (2%)
    ppermute x24, starting transfers between devices, along(): return lax.ppermute(block, ('z', 'c'), route)  71.9 us
    ppermute x24, waiting for transfers between devices, along(): return lax.ppermute(block, ('z', 'c'), route)  69.6 us
    ppermute x9, starting transfers between devices, swap(): return lax.ppermute(block, axis, [(0, 1), (1, 0)])  20.2 us
    dot_general x20, matrix products, dot(): lax.dot_general(left, right, (((left_dim,), (right_dim,)), ((), ())), pre...  11.6 us
    ppermute x1, waiting for transfers between devices, section(): lax.ppermute(grad_bf[None], 'pipe', [(i, i - 1) for i in range(1, section...  7.2 us
  transfers between devices with their start and end apart: 34, of which 18 were waited for; matrix products, arithmetic and copies ran while one was open for 7% of the time, Pallas kernels for 0%

profile of v3, /device:TPU:24, one launch (start us, length us, event | category | flops | bytes accessed | tf_op | source)
XLA Modules:
  0.0 193.6 jit_solution(5964414030971645332)
XLA Ops:
  3.4 1.9 collective-permute-start.9
  5.4 2.4 %collective-permute-start = (bf16[12,3584]{1,0:T(8,128)(2,1)}, bf16[12,3584]{1,0:T(8,128)(2,1)S(1)}, u32[]{:S(2)}, u32[]{:S(2)}) collective-permute-start(bf16[12,3584]{1,0:T(8,128)(2,1)} %bitcast.47), channel_id=1, source_target_pairs={{0,1},{1,0},{2,3},{3,2},{4,5},{5,4},{6,7},{7,6},{8,9},{9,8},{10,11... | collective-permute-start | bytes 258056 | tf_op jit(solution)/shard_map/ppermute | solution.py:13
  7.8 3.4 %collective-permute-start.20 = (bf16[256,3584]{1,0:T(8,128)(2,1)}, bf16[256,3584]{1,0:T(8,128)(2,1)}, u32[]{:S(2)}, u32[]{:S(2)}) collective-permute-start(bf16[256,3584]{1,0:T(8,128)(2,1)} %bitcast.51), channel_id=1, source_target_pairs={{0,2},{2,0},{1,3},{3,1},{4,6},{6,4},{5,7},{7,5},{8,10},{10,8},{9,1... | collective-permute-start | bytes 5505032 | tf_op jit(solution)/shard_map/ppermute | solution.py:13
  12.2 4.0 %collective-permute-start.1 = (bf16[24,3584]{1,0:T(8,128)(2,1)S(1)}, bf16[24,3584]{1,0:T(8,128)(2,1)S(1)}, u32[]{:S(2)}, u32[]{:S(2)}) collective-permute-start(bf16[24,3584]{1,0:T(8,128)(2,1)S(1)} %pad_maximum_fusion.2), channel_id=1, source_target_pairs={{0,4},{1,61},{4,8},{5,1},{8,12},{9,5},{12,16},{13,9},{16,20},{17,1... | collective-permute-start | bytes 516104 | tf_op jit(solution)/shard_map/ppermute | solution.py:23
  17.2 3.8 %collective-permute-start.10 = (bf16[24,3712]{1,0:T(8,128)(2,1)S(1)}, bf16[24,3712]{1,0:T(8,128)(2,1)S(1)}, u32[]{:S(2)}, u32[]{:S(2)}) collective-permute-start(bf16[24,3712]{1,0:T(8,128)(2,1)S(1)} %pad_maximum_fusion.1), channel_id=1, source_target_pairs={{0,4},{1,61},{4,8},{5,1},{8,12},{9,5},{12,16},{13,9},{16,20},{17,1... | collective-permute-start | bytes 534536 | tf_op jit(solution)/shard_map/ppermute | solution.py:23
  21.1 6.1 %collective-permute-done.1 = bf16[24,3584]{1,0:T(8,128)(2,1)S(1)} collective-permute-done((bf16[24,3584]{1,0:T(8,128)(2,1)S(1)}, bf16[24,3584]{1,0:T(8,128)(2,1)S(1)}, u32[]{:S(2)}, u32[]{:S(2)}) %collective-permute-start.1) | collective-permute-done | bytes 172064 | tf_op jit(solution)/shard_map/ppermute | solution.py:23
  27.2 1.9 collective-permute-start.2
  30.2 2.4 %collective-permute-start.21 = (bf16[3584,256]{1,0:T(8,128)(2,1)S(1)}, bf16[3584,256]{1,0:T(8,128)(2,1)S(1)}, u32[]{:S(2)}, u32[]{:S(2)}) collective-permute-start(bf16[3584,256]{1,0:T(8,128)(2,1)S(1)} %bitcast.43), channel_id=1, source_target_pairs={{0,2},{2,0},{1,3},{3,1},{4,6},{6,4},{5,7},{7,5},{8,10},{10,8},{9,1... | collective-permute-start | bytes 5505032 | tf_op jit(solution)/shard_map/ppermute | solution.py:13
  32.6 1.9 collective-permute-start.11
  35.7 1.9 collective-permute-start.3
  37.6 3.6 %collective-permute-done.11 = bf16[24,3712]{1,0:T(8,128)(2,1)S(1)} collective-permute-done((bf16[24,3712]{1,0:T(8,128)(2,1)S(1)}, bf16[24,3712]{1,0:T(8,128)(2,1)S(1)}, u32[]{:S(2)}, u32[]{:S(2)}) %collective-permute-start.11) | collective-permute-done | bytes 178208 | tf_op jit(solution)/shard_map/ppermute | solution.py:23
  41.2 1.9 collective-permute-start.12
  44.2 1.9 collective-permute-start.4
  46.1 3.7 %collective-permute-done.12 = bf16[24,3712]{1,0:T(8,128)(2,1)S(1)} collective-permute-done((bf16[24,3712]{1,0:T(8,128)(2,1)S(1)}, bf16[24,3712]{1,0:T(8,128)(2,1)S(1)}, u32[]{:S(2)}, u32[]{:S(2)}) %collective-permute-start.12) | collective-permute-done | bytes 178208 | tf_op jit(solution)/shard_map/ppermute | solution.py:23
  49.8 1.9 collective-permute-start.18
  51.7 1.9 collective-permute-start.13
  53.6 1.9 collective-permute-start.5
  55.6 4.7 %collective-permute-done.13 = bf16[24,3712]{1,0:T(8,128)(2,1)S(1)} collective-permute-done((bf16[24,3712]{1,0:T(8,128)(2,1)S(1)}, bf16[24,3712]{1,0:T(8,128)(2,1)S(1)}, u32[]{:S(2)}, u32[]{:S(2)}) %collective-permute-start.13) | collective-permute-done | bytes 178208 | tf_op jit(solution)/shard_map/ppermute | solution.py:23
  60.3 1.9 collective-permute-start.14
  62.2 1.9 collective-permute-start.6
  64.2 4.7 %collective-permute-done.14 = bf16[24,3712]{1,0:T(8,128)(2,1)S(1)} collective-permute-done((bf16[24,3712]{1,0:T(8,128)(2,1)S(1)}, bf16[24,3712]{1,0:T(8,128)(2,1)S(1)}, u32[]{:S(2)}, u32[]{:S(2)}) %collective-permute-start.14) | collective-permute-done | bytes 178208 | tf_op jit(solution)/shard_map/ppermute | solution.py:23
  68.8 1.9 collective-permute-start.19
  70.8 1.9 collective-permute-start.15
  72.7 6.6 %collective-permute-done.15 = bf16[24,3712]{1,0:T(8,128)(2,1)S(1)} collective-permute-done((bf16[24,3712]{1,0:T(8,128)(2,1)S(1)}, bf16[24,3712]{1,0:T(8,128)(2,1)S(1)}, u32[]{:S(2)}, u32[]{:S(2)}) %collective-permute-start.15) | collective-permute-done | bytes 178208 | tf_op jit(solution)/shard_map/ppermute | solution.py:23
  79.3 1.9 collective-permute-start.7
  81.3 6.6 %collective-permute-done.7 = bf16[24,3584]{1,0:T(8,128)(2,1)S(1)} collective-permute-done((bf16[24,3584]{1,0:T(8,128)(2,1)S(1)}, bf16[24,3584]{1,0:T(8,128)(2,1)S(1)}, u32[]{:S(2)}, u32[]{:S(2)}) %collective-permute-start.7) | collective-permute-done | bytes 172064 | tf_op jit(solution)/shard_map/ppermute | solution.py:23
  87.8 1.9 collective-permute-start.16
  89.8 6.6 %collective-permute-done.16 = bf16[24,3712]{1,0:T(8,128)(2,1)S(1)} collective-permute-done((bf16[24,3712]{1,0:T(8,128)(2,1)S(1)}, bf16[24,3712]{1,0:T(8,128)(2,1)S(1)}, u32[]{:S(2)}, u32[]{:S(2)}) %collective-permute-start.16) | collective-permute-done | bytes 178208 | tf_op jit(solution)/shard_map/ppermute | solution.py:23
  96.4 1.9 collective-permute-start.8
  98.4 6.6 %collective-permute-done.8 = bf16[24,3584]{1,0:T(8,128)(2,1)S(1)} collective-permute-done((bf16[24,3584]{1,0:T(8,128)(2,1)S(1)}, bf16[24,3584]{1,0:T(8,128)(2,1)S(1)}, u32[]{:S(2)}, u32[]{:S(2)}) %collective-permute-start.8) | collective-permute-done | bytes 172064 | tf_op jit(solution)/shard_map/ppermute | solution.py:23
  104.9 1.9 collective-permute-start.17
  106.9 6.6 %collective-permute-done.17 = bf16[24,3712]{1,0:T(8,128)(2,1)S(1)} collective-permute-done((bf16[24,3712]{1,0:T(8,128)(2,1)S(1)}, bf16[24,3712]{1,0:T(8,128)(2,1)S(1)}, u32[]{:S(2)}, u32[]{:S(2)}) %collective-permute-start.17) | collective-permute-done | bytes 178208 | tf_op jit(solution)/shard_map/ppermute | solution.py:23
  116.2 1.9 collective-permute-start.22
  118.2 2.4 %collective-permute-start.23 = (bf16[3584,256]{1,0:T(8,128)(2,1)S(1)}, bf16[3584,256]{1,0:T(8,128)(2,1)S(1)}, u32[]{:S(2)}, u32[]{:S(2)}) collective-permute-start(bf16[3584,256]{1,0:T(8,128)(2,1)S(1)} %collective-permute-done.21), channel_id=1, source_target_pairs={{0,1},{1,0},{2,3},{3,2},{4,5},{5,4},{6,7},{7,6},{8,9},{9,8},{10,11... | collective-permute-start | bytes 5505032 | tf_op jit(solution)/shard_map/ppermute | solution.py:13
  123.8 2.3 %multiply_convert_fusion.1 = (bf16[192,256]{1,0:T(8,128)(2,1)S(1)}, f32[192]{0:T(256)S(1)}) fusion(f32[192,256]{1,0:T(8,128)S(1)} %convolution_add_fusion.5, bf16[192,3584]{1,0:T(8,128)(2,1)S(1)} %select_dynamic-update-slice_fusion.1, bf16[256,3584]{1,0:T(8,128)(2,1)} %collective-permute-done.20), kind=kOutput, calls=%fused_computation.63 | convolution fusion | flops 352911168 | bytes 3506944 | tf_op jit(solution)/shard_map/dot_general | solution.py:87
  130.1 2.2 %collective-permute-start.24 = (bf16[24,3712]{1,0:T(8,128)(2,1)S(1)}, bf16[24,3712]{1,0:T(8,128)(2,1)S(1)}, u32[]{:S(2)}, u32[]{:S(2)}) collective-permute-start(bf16[24,3712]{1,0:T(8,128)(2,1)S(1)} %get-tuple-element.32), channel_id=1, source_target_pairs={{0,56},{4,60},{8,0},{12,4},{16,8},{20,12},{24,16},{28,20},{32,24},... | collective-permute-start | bytes 534536 | tf_op jit(solution)/shard_map/ppermute | solution.py:23
  132.3 7.8 %collective-permute-start.28 = (bf16[24,3712]{1,0:T(8,128)(2,1)S(1)}, bf16[24,3712]{1,0:T(8,128)(2,1)S(1)}, u32[]{:S(2)}, u32[]{:S(2)}) collective-permute-start(bf16[24,3712]{1,0:T(8,128)(2,1)S(1)} %get-tuple-element.28), channel_id=1, source_target_pairs={{0,56},{1,9},{4,60},{5,13},{8,0},{9,17},{12,4},{13,21},{16,8},{17,... | collective-permute-start | bytes 534536 | tf_op jit(solution)/shard_map/ppermute | solution.py:23
  140.1 3.7 %collective-permute-start.25 = (bf16[24,3712]{1,0:T(8,128)(2,1)S(1)}, bf16[24,3712]{1,0:T(8,128)(2,1)S(1)}, u32[]{:S(2)}, u32[]{:S(2)}) collective-permute-start(bf16[24,3712]{1,0:T(8,128)(2,1)S(1)} %add_convert_fusion.5), channel_id=1, source_target_pairs={{0,56},{1,9},{4,60},{5,13},{8,0},{9,17},{12,4},{13,21},{16,8},{17,... | collective-permute-start | bytes 534536 | tf_op jit(solution)/shard_map/ppermute | solution.py:23
  143.9 5.9 %collective-permute-start.29 = (bf16[24,3712]{1,0:T(8,128)(2,1)S(1)}, bf16[24,3712]{1,0:T(8,128)(2,1)S(1)}, u32[]{:S(2)}, u32[]{:S(2)}) collective-permute-start(bf16[24,3712]{1,0:T(8,128)(2,1)S(1)} %add_convert_fusion.2), channel_id=1, source_target_pairs={{0,56},{1,9},{4,60},{5,13},{8,0},{9,17},{12,4},{13,21},{16,8},{17,... | collective-permute-start | bytes 534536 | tf_op jit(solution)/shard_map/ppermute | solution.py:23
  149.9 4.1 %collective-permute-start.26 = (bf16[24,3712]{1,0:T(8,128)(2,1)S(1)}, bf16[24,3712]{1,0:T(8,128)(2,1)S(1)}, u32[]{:S(2)}, u32[]{:S(2)}) collective-permute-start(bf16[24,3712]{1,0:T(8,128)(2,1)S(1)} %add_convert_fusion.4), channel_id=1, source_target_pairs={{0,56},{1,9},{4,60},{5,13},{8,0},{9,17},{12,4},{13,21},{16,8},{17,... | collective-permute-start | bytes 534536 | tf_op jit(solution)/shard_map/ppermute | solution.py:23
  154.1 5.9 %collective-permute-start.30 = (bf16[24,3712]{1,0:T(8,128)(2,1)S(1)}, bf16[24,3712]{1,0:T(8,128)(2,1)S(1)}, u32[]{:S(2)}, u32[]{:S(2)}) collective-permute-start(bf16[24,3712]{1,0:T(8,128)(2,1)S(1)} %add_convert_fusion.1), channel_id=1, source_target_pairs={{0,56},{1,9},{4,60},{5,13},{8,0},{9,17},{12,4},{13,21},{16,8},{17,... | collective-permute-start | bytes 534536 | tf_op jit(solution)/shard_map/ppermute | solution.py:23
  160.1 4.2 %collective-permute-done.30 = bf16[24,3712]{1,0:T(8,128)(2,1)S(1)} collective-permute-done((bf16[24,3712]{1,0:T(8,128)(2,1)S(1)}, bf16[24,3712]{1,0:T(8,128)(2,1)S(1)}, u32[]{:S(2)}, u32[]{:S(2)}) %collective-permute-start.30) | collective-permute-done | bytes 178208 | tf_op jit(solution)/shard_map/ppermute | solution.py:23
  164.3 5.8 %collective-permute-start.31 = (bf16[24,3712]{1,0:T(8,128)(2,1)S(1)}, bf16[24,3712]{1,0:T(8,128)(2,1)S(1)}, u32[]{:S(2)}, u32[]{:S(2)}) collective-permute-start(bf16[24,3712]{1,0:T(8,128)(2,1)S(1)} %add_convert_fusion), channel_id=1, source_target_pairs={{0,60},{1,5},{4,0},{5,9},{8,4},{9,13},{12,8},{13,17},{16,12},{17,2... | collective-permute-start | bytes 534536 | tf_op jit(solution)/shard_map/ppermute | solution.py:23
  170.1 1.9 collective-permute-start.27
  173.1 5.5 %collective-permute-done.27 = bf16[24,3712]{1,0:T(8,128)(2,1)S(1)} collective-permute-done((bf16[24,3712]{1,0:T(8,128)(2,1)S(1)}, bf16[24,3712]{1,0:T(8,128)(2,1)S(1)}, u32[]{:S(2)}, u32[]{:S(2)}) %collective-permute-start.27) | collective-permute-done | bytes 178208 | tf_op jit(solution)/shard_map/ppermute | solution.py:23
  178.8 1.9 collective-permute-start.32
  182.3 2.6 %collective-permute-start.33 = (bf16[1,12,3584]{2,1,0:T(8,128)(2,1)S(1)}, bf16[1,12,3584]{2,1,0:T(8,128)(2,1)S(1)}, u32[]{:S(2)}, u32[]{:S(2)}) collective-permute-start(bf16[1,12,3584]{2,1,0:T(8,128)(2,1)S(1)} %fusion.40), channel_id=1, source_target_pairs={{64,0},{128,64},{192,128},{256,192},{320,256},{384,320},{448,384},... | collective-permute-start | bytes 258056 | tf_op jit(solution)/shard_map/ppermute | solution.py:139
  185.8 7.2 %collective-permute-done.33 = bf16[1,12,3584]{2,1,0:T(8,128)(2,1)S(1)} collective-permute-done((bf16[1,12,3584]{2,1,0:T(8,128)(2,1)S(1)}, bf16[1,12,3584]{2,1,0:T(8,128)(2,1)S(1)}, u32[]{:S(2)}, u32[]{:S(2)}) %collective-permute-start.33) | collective-permute-done | bytes 86048 | tf_op jit(solution)/shard_map/ppermute | solution.py:139
  (93 shorter events, 22.6 us)
Async XLA Ops:
  0.6 29.5 %copy-start = (bf16[1,3584,256]{2,1,0:T(8,128)(2,1)S(1)}, bf16[1,3584,256]{2,1,0:T(8,128)(2,1)}, u32[]{:S(2)}) copy-start(bf16[1,3584,256]{2,1,0:T(8,128)(2,1)} %param.10) | copy-start | bytes 5505028
  3.4 12.8 %collective-permute-start.9 = (bf16[12,3712]{1,0:T(8,128)(2,1)S(1)}, bf16[12,3712]{1,0:T(8,128)(2,1)S(1)}, u32[]{:S(2)}, u32[]{:S(2)}) collective-permute-start(bf16[12,3712]{1,0:T(8,128)(2,1)S(1)} %pad_maximum_fusion.3), channel_id=1, source_target_pairs={{0,1},{1,0},{2,3},{3,2},{4,5},{5,4},{6,7},{7,6},{8,9},{9,8},{10,11... | collective-permute-start | bytes 267272 | tf_op jit(solution)/shard_map/ppermute | solution.py:13
  5.4 5.9 %collective-permute-start = (bf16[12,3584]{1,0:T(8,128)(2,1)}, bf16[12,3584]{1,0:T(8,128)(2,1)S(1)}, u32[]{:S(2)}, u32[]{:S(2)}) collective-permute-start(bf16[12,3584]{1,0:T(8,128)(2,1)} %bitcast.47), channel_id=1, source_target_pairs={{0,1},{1,0},{2,3},{3,2},{4,5},{5,4},{6,7},{7,6},{8,9},{9,8},{10,11... | collective-permute-start | bytes 258056 | tf_op jit(solution)/shard_map/ppermute | solution.py:13
  7.8 108.4 %collective-permute-start.20 = (bf16[256,3584]{1,0:T(8,128)(2,1)}, bf16[256,3584]{1,0:T(8,128)(2,1)}, u32[]{:S(2)}, u32[]{:S(2)}) collective-permute-start(bf16[256,3584]{1,0:T(8,128)(2,1)} %bitcast.51), channel_id=1, source_target_pairs={{0,2},{2,0},{1,3},{3,1},{4,6},{6,4},{5,7},{7,5},{8,10},{10,8},{9,1... | collective-permute-start | bytes 5505032 | tf_op jit(solution)/shard_map/ppermute | solution.py:13
  12.2 37.6 %copy-start.1 = (bf16[1,256,3584]{2,1,0:T(8,128)(2,1)S(1)}, bf16[1,256,3584]{2,1,0:T(8,128)(2,1)}, u32[]{:S(2)}) copy-start(bf16[1,256,3584]{2,1,0:T(8,128)(2,1)} %param.11) | copy-start | bytes 5505028
  12.2 14.9 %collective-permute-start.1 = (bf16[24,3584]{1,0:T(8,128)(2,1)S(1)}, bf16[24,3584]{1,0:T(8,128)(2,1)S(1)}, u32[]{:S(2)}, u32[]{:S(2)}) collective-permute-start(bf16[24,3584]{1,0:T(8,128)(2,1)S(1)} %pad_maximum_fusion.2), channel_id=1, source_target_pairs={{0,4},{1,61},{4,8},{5,1},{8,12},{9,5},{12,16},{13,9},{16,20},{17,1... | collective-permute-start | bytes 516104 | tf_op jit(solution)/shard_map/ppermute | solution.py:23
  17.2 12.9 %collective-permute-start.10 = (bf16[24,3712]{1,0:T(8,128)(2,1)S(1)}, bf16[24,3712]{1,0:T(8,128)(2,1)S(1)}, u32[]{:S(2)}, u32[]{:S(2)}) collective-permute-start(bf16[24,3712]{1,0:T(8,128)(2,1)S(1)} %pad_maximum_fusion.1), channel_id=1, source_target_pairs={{0,4},{1,61},{4,8},{5,1},{8,12},{9,5},{12,16},{13,9},{16,20},{17,1... | collective-permute-start | bytes 534536 | tf_op jit(solution)/shard_map/ppermute | solution.py:23
  27.2 8.5 %collective-permute-start.2 = (bf16[24,3584]{1,0:T(8,128)(2,1)S(1)}, bf16[24,3584]{1,0:T(8,128)(2,1)S(1)}, u32[]{:S(2)}, u32[]{:S(2)}) collective-permute-start(bf16[24,3584]{1,0:T(8,128)(2,1)S(1)} %collective-permute-done.1), channel_id=1, source_target_pairs={{0,4},{1,61},{4,8},{5,1},{8,12},{9,5},{12,16},{13,9},{16,20},{17,1... | collective-permute-start | bytes 516104 | tf_op jit(solution)/shard_map/ppermute | solution.py:23
  30.2 88.0 %collective-permute-start.21 = (bf16[3584,256]{1,0:T(8,128)(2,1)S(1)}, bf16[3584,256]{1,0:T(8,128)(2,1)S(1)}, u32[]{:S(2)}, u32[]{:S(2)}) collective-permute-start(bf16[3584,256]{1,0:T(8,128)(2,1)S(1)} %bitcast.43), channel_id=1, source_target_pairs={{0,2},{2,0},{1,3},{3,1},{4,6},{6,4},{5,7},{7,5},{8,10},{10,8},{9,1... | collective-permute-start | bytes 5505032 | tf_op jit(solution)/shard_map/ppermute | solution.py:13
  32.6 8.6 %collective-permute-start.11 = (bf16[24,3712]{1,0:T(8,128)(2,1)S(1)}, bf16[24,3712]{1,0:T(8,128)(2,1)S(1)}, u32[]{:S(2)}, u32[]{:S(2)}) collective-permute-start(bf16[24,3712]{1,0:T(8,128)(2,1)S(1)} %collective-permute-done.10), channel_id=1, source_target_pairs={{0,4},{1,61},{4,8},{5,1},{8,12},{9,5},{12,16},{13,9},{16,20},{17,1... | collective-permute-start | bytes 534536 | tf_op jit(solution)/shard_map/ppermute | solution.py:23
  35.7 8.5 %collective-permute-start.3 = (bf16[24,3584]{1,0:T(8,128)(2,1)S(1)}, bf16[24,3584]{1,0:T(8,128)(2,1)S(1)}, u32[]{:S(2)}, u32[]{:S(2)}) collective-permute-start(bf16[24,3584]{1,0:T(8,128)(2,1)S(1)} %collective-permute-done.2), channel_id=1, source_target_pairs={{0,4},{1,61},{4,8},{5,1},{8,12},{9,5},{12,16},{13,9},{16,20},{17,1... | collective-permute-start | bytes 516104 | tf_op jit(solution)/shard_map/ppermute | solution.py:23
  41.2 8.6 %collective-permute-start.12 = (bf16[24,3712]{1,0:T(8,128)(2,1)S(1)}, bf16[24,3712]{1,0:T(8,128)(2,1)S(1)}, u32[]{:S(2)}, u32[]{:S(2)}) collective-permute-start(bf16[24,3712]{1,0:T(8,128)(2,1)S(1)} %collective-permute-done.11), channel_id=1, source_target_pairs={{0,4},{1,61},{4,8},{5,1},{8,12},{9,5},{12,16},{13,9},{16,20},{17,1... | collective-permute-start | bytes 534536 | tf_op jit(solution)/shard_map/ppermute | solution.py:23
  44.2 9.5 %collective-permute-start.4 = (bf16[24,3584]{1,0:T(8,128)(2,1)S(1)}, bf16[24,3584]{1,0:T(8,128)(2,1)S(1)}, u32[]{:S(2)}, u32[]{:S(2)}) collective-permute-start(bf16[24,3584]{1,0:T(8,128)(2,1)S(1)} %collective-permute-done.3), channel_id=1, source_target_pairs={{0,4},{1,61},{4,8},{5,1},{8,12},{9,5},{12,16},{13,9},{16,20},{17,1... | collective-permute-start | bytes 516104 | tf_op jit(solution)/shard_map/ppermute | solution.py:23
  49.8 71.5 %collective-permute-start.18 = (bf16[256,3584]{1,0:T(8,128)(2,1)S(1)}, bf16[256,3584]{1,0:T(8,128)(2,1)S(1)}, u32[]{:S(2)}, u32[]{:S(2)}) collective-permute-start(bf16[256,3584]{1,0:T(8,128)(2,1)S(1)} %bitcast.52), channel_id=1, source_target_pairs={{0,1},{1,0},{2,3},{3,2},{4,5},{5,4},{6,7},{7,6},{8,9},{9,8},{10,11... | collective-permute-start | bytes 5505032 | tf_op jit(solution)/shard_map/ppermute | solution.py:13
  51.7 8.6 %collective-permute-start.13 = (bf16[24,3712]{1,0:T(8,128)(2,1)S(1)}, bf16[24,3712]{1,0:T(8,128)(2,1)S(1)}, u32[]{:S(2)}, u32[]{:S(2)}) collective-permute-start(bf16[24,3712]{1,0:T(8,128)(2,1)S(1)} %collective-permute-done.12), channel_id=1, source_target_pairs={{0,4},{1,61},{4,8},{5,1},{8,12},{9,5},{12,16},{13,9},{16,20},{17,1... | collective-permute-start | bytes 534536 | tf_op jit(solution)/shard_map/ppermute | solution.py:23
  53.6 8.6 %collective-permute-start.5 = (bf16[24,3584]{1,0:T(8,128)(2,1)S(1)}, bf16[24,3584]{1,0:T(8,128)(2,1)S(1)}, u32[]{:S(2)}, u32[]{:S(2)}) collective-permute-start(bf16[24,3584]{1,0:T(8,128)(2,1)S(1)} %collective-permute-done.4), channel_id=1, source_target_pairs={{0,4},{1,61},{4,8},{5,1},{8,12},{9,5},{12,16},{13,9},{16,20},{17,1... | collective-permute-start | bytes 516104 | tf_op jit(solution)/shard_map/ppermute | solution.py:23
  60.3 8.6 %collective-permute-start.14 = (bf16[24,3712]{1,0:T(8,128)(2,1)S(1)}, bf16[24,3712]{1,0:T(8,128)(2,1)S(1)}, u32[]{:S(2)}, u32[]{:S(2)}) collective-permute-start(bf16[24,3712]{1,0:T(8,128)(2,1)S(1)} %collective-permute-done.13), channel_id=1, source_target_pairs={{0,4},{1,61},{4,8},{5,1},{8,12},{9,5},{12,16},{13,9},{16,20},{17,1... | collective-permute-start | bytes 534536 | tf_op jit(solution)/shard_map/ppermute | solution.py:23
  62.2 8.6 %collective-permute-start.6 = (bf16[24,3584]{1,0:T(8,128)(2,1)S(1)}, bf16[24,3584]{1,0:T(8,128)(2,1)S(1)}, u32[]{:S(2)}, u32[]{:S(2)}) collective-permute-start(bf16[24,3584]{1,0:T(8,128)(2,1)S(1)} %collective-permute-done.5), channel_id=1, source_target_pairs={{0,4},{1,61},{4,8},{5,1},{8,12},{9,5},{12,16},{13,9},{16,20},{17,1... | collective-permute-start | bytes 516104 | tf_op jit(solution)/shard_map/ppermute | solution.py:23
  68.8 51.8 %collective-permute-start.19 = (bf16[3584,256]{1,0:T(8,128)(2,1)S(1)}, bf16[3584,256]{1,0:T(8,128)(2,1)S(1)}, u32[]{:S(2)}, u32[]{:S(2)}) collective-permute-start(bf16[3584,256]{1,0:T(8,128)(2,1)S(1)} %bitcast.44), channel_id=1, source_target_pairs={{0,1},{1,0},{2,3},{3,2},{4,5},{5,4},{6,7},{7,6},{8,9},{9,8},{10,11... | collective-permute-start | bytes 5505032 | tf_op jit(solution)/shard_map/ppermute | solution.py:13
  70.8 8.6 %collective-permute-start.15 = (bf16[24,3712]{1,0:T(8,128)(2,1)S(1)}, bf16[24,3712]{1,0:T(8,128)(2,1)S(1)}, u32[]{:S(2)}, u32[]{:S(2)}) collective-permute-start(bf16[24,3712]{1,0:T(8,128)(2,1)S(1)} %collective-permute-done.14), channel_id=1, source_target_pairs={{0,4},{1,61},{4,8},{5,1},{8,12},{9,5},{12,16},{13,9},{16,20},{17,1... | collective-permute-start | bytes 534536 | tf_op jit(solution)/shard_map/ppermute | solution.py:23
  79.3 8.5 %collective-permute-start.7 = (bf16[24,3584]{1,0:T(8,128)(2,1)S(1)}, bf16[24,3584]{1,0:T(8,128)(2,1)S(1)}, u32[]{:S(2)}, u32[]{:S(2)}) collective-permute-start(bf16[24,3584]{1,0:T(8,128)(2,1)S(1)} %collective-permute-done.6), channel_id=1, source_target_pairs={{0,4},{1,61},{4,8},{5,1},{8,12},{9,5},{12,16},{13,9},{16,20},{17,1... | collective-permute-start | bytes 516104 | tf_op jit(solution)/shard_map/ppermute | solution.py:23
  87.8 8.6 %collective-permute-start.16 = (bf16[24,3712]{1,0:T(8,128)(2,1)S(1)}, bf16[24,3712]{1,0:T(8,128)(2,1)S(1)}, u32[]{:S(2)}, u32[]{:S(2)}) collective-permute-start(bf16[24,3712]{1,0:T(8,128)(2,1)S(1)} %collective-permute-done.15), channel_id=1, source_target_pairs={{0,4},{1,61},{4,8},{5,1},{8,12},{9,5},{12,16},{13,9},{16,20},{17,1... | collective-permute-start | bytes 534536 | tf_op jit(solution)/shard_map/ppermute | solution.py:23
  96.4 8.5 %collective-permute-start.8 = (bf16[24,3584]{1,0:T(8,128)(2,1)S(1)}, bf16[24,3584]{1,0:T(8,128)(2,1)S(1)}, u32[]{:S(2)}, u32[]{:S(2)}) collective-permute-start(bf16[24,3584]{1,0:T(8,128)(2,1)S(1)} %collective-permute-done.7), channel_id=1, source_target_pairs={{0,4},{4,8},{8,12},{12,16},{16,20},{20,24},{24,28},{28,32},{32,36}... | collective-permute-start | bytes 516104 | tf_op jit(solution)/shard_map/ppermute | solution.py:23
  104.9 8.6 %collective-permute-start.17 = (bf16[24,3712]{1,0:T(8,128)(2,1)S(1)}, bf16[24,3712]{1,0:T(8,128)(2,1)S(1)}, u32[]{:S(2)}, u32[]{:S(2)}) collective-permute-start(bf16[24,3712]{1,0:T(8,128)(2,1)S(1)} %collective-permute-done.16), channel_id=1, source_target_pairs={{0,4},{4,8},{8,12},{12,16},{16,20},{20,24},{24,28},{28,32},{32,36}... | collective-permute-start | bytes 534536 | tf_op jit(solution)/shard_map/ppermute | solution.py:23
  116.2 11.0 %collective-permute-start.22 = (bf16[256,3584]{1,0:T(8,128)(2,1)}, bf16[256,3584]{1,0:T(8,128)(2,1)S(1)}, u32[]{:S(2)}, u32[]{:S(2)}) collective-permute-start(bf16[256,3584]{1,0:T(8,128)(2,1)} %collective-permute-done.20), channel_id=1, source_target_pairs={{0,1},{1,0},{2,3},{3,2},{4,5},{5,4},{6,7},{7,6},{8,9},{9,8},{10,11... | collective-permute-start | bytes 5505032 | tf_op jit(solution)/shard_map/ppermute | solution.py:13
  118.2 9.0 %collective-permute-start.23 = (bf16[3584,256]{1,0:T(8,128)(2,1)S(1)}, bf16[3584,256]{1,0:T(8,128)(2,1)S(1)}, u32[]{:S(2)}, u32[]{:S(2)}) collective-permute-start(bf16[3584,256]{1,0:T(8,128)(2,1)S(1)} %collective-permute-done.21), channel_id=1, source_target_pairs={{0,1},{1,0},{2,3},{3,2},{4,5},{5,4},{6,7},{7,6},{8,9},{9,8},{10,11... | collective-permute-start | bytes 5505032 | tf_op jit(solution)/shard_map/ppermute | solution.py:13
  130.1 10.0 %collective-permute-start.24 = (bf16[24,3712]{1,0:T(8,128)(2,1)S(1)}, bf16[24,3712]{1,0:T(8,128)(2,1)S(1)}, u32[]{:S(2)}, u32[]{:S(2)}) collective-permute-start(bf16[24,3712]{1,0:T(8,128)(2,1)S(1)} %get-tuple-element.32), channel_id=1, source_target_pairs={{0,56},{4,60},{8,0},{12,4},{16,8},{20,12},{24,16},{28,20},{32,24},... | collective-permute-start | bytes 534536 | tf_op jit(solution)/shard_map/ppermute | solution.py:23
  132.3 11.5 %collective-permute-start.28 = (bf16[24,3712]{1,0:T(8,128)(2,1)S(1)}, bf16[24,3712]{1,0:T(8,128)(2,1)S(1)}, u32[]{:S(2)}, u32[]{:S(2)}) collective-permute-start(bf16[24,3712]{1,0:T(8,128)(2,1)S(1)} %get-tuple-element.28), channel_id=1, source_target_pairs={{0,56},{1,9},{4,60},{5,13},{8,0},{9,17},{12,4},{13,21},{16,8},{17,... | collective-permute-start | bytes 534536 | tf_op jit(solution)/shard_map/ppermute | solution.py:23
  140.1 9.7 %collective-permute-start.25 = (bf16[24,3712]{1,0:T(8,128)(2,1)S(1)}, bf16[24,3712]{1,0:T(8,128)(2,1)S(1)}, u32[]{:S(2)}, u32[]{:S(2)}) collective-permute-start(bf16[24,3712]{1,0:T(8,128)(2,1)S(1)} %add_convert_fusion.5), channel_id=1, source_target_pairs={{0,56},{1,9},{4,60},{5,13},{8,0},{9,17},{12,4},{13,21},{16,8},{17,... | collective-permute-start | bytes 534536 | tf_op jit(solution)/shard_map/ppermute | solution.py:23
  143.9 10.2 %collective-permute-start.29 = (bf16[24,3712]{1,0:T(8,128)(2,1)S(1)}, bf16[24,3712]{1,0:T(8,128)(2,1)S(1)}, u32[]{:S(2)}, u32[]{:S(2)}) collective-permute-start(bf16[24,3712]{1,0:T(8,128)(2,1)S(1)} %add_convert_fusion.2), channel_id=1, source_target_pairs={{0,56},{1,9},{4,60},{5,13},{8,0},{9,17},{12,4},{13,21},{16,8},{17,... | collective-permute-start | bytes 534536 | tf_op jit(solution)/shard_map/ppermute | solution.py:23
  149.9 10.1 %collective-permute-start.26 = (bf16[24,3712]{1,0:T(8,128)(2,1)S(1)}, bf16[24,3712]{1,0:T(8,128)(2,1)S(1)}, u32[]{:S(2)}, u32[]{:S(2)}) collective-permute-start(bf16[24,3712]{1,0:T(8,128)(2,1)S(1)} %add_convert_fusion.4), channel_id=1, source_target_pairs={{0,56},{1,9},{4,60},{5,13},{8,0},{9,17},{12,4},{13,21},{16,8},{17,... | collective-permute-start | bytes 534536 | tf_op jit(solution)/shard_map/ppermute | solution.py:23
  154.1 10.2 %collective-permute-start.30 = (bf16[24,3712]{1,0:T(8,128)(2,1)S(1)}, bf16[24,3712]{1,0:T(8,128)(2,1)S(1)}, u32[]{:S(2)}, u32[]{:S(2)}) collective-permute-start(bf16[24,3712]{1,0:T(8,128)(2,1)S(1)} %add_convert_fusion.1), channel_id=1, source_target_pairs={{0,56},{1,9},{4,60},{5,13},{8,0},{9,17},{12,4},{13,21},{16,8},{17,... | collective-permute-start | bytes 534536 | tf_op jit(solution)/shard_map/ppermute | solution.py:23
  164.3 8.8 %collective-permute-start.31 = (bf16[24,3712]{1,0:T(8,128)(2,1)S(1)}, bf16[24,3712]{1,0:T(8,128)(2,1)S(1)}, u32[]{:S(2)}, u32[]{:S(2)}) collective-permute-start(bf16[24,3712]{1,0:T(8,128)(2,1)S(1)} %add_convert_fusion), channel_id=1, source_target_pairs={{0,60},{1,5},{4,0},{5,9},{8,4},{9,13},{12,8},{13,17},{16,12},{17,2... | collective-permute-start | bytes 534536 | tf_op jit(solution)/shard_map/ppermute | solution.py:23
  170.1 8.5 %collective-permute-start.27 = (bf16[24,3712]{1,0:T(8,128)(2,1)S(1)}, bf16[24,3712]{1,0:T(8,128)(2,1)S(1)}, u32[]{:S(2)}, u32[]{:S(2)}) collective-permute-start(bf16[24,3712]{1,0:T(8,128)(2,1)S(1)} %add_convert_fusion.3), channel_id=1, source_target_pairs={{0,56},{1,9},{4,60},{5,13},{8,0},{9,17},{12,4},{13,21},{16,8},{17,... | collective-permute-start | bytes 534536 | tf_op jit(solution)/shard_map/ppermute | solution.py:23
  178.8 3.4 %collective-permute-start.32 = (f32[12,3712]{1,0:T(8,128)S(1)}, f32[12,3712]{1,0:T(8,128)S(1)}, u32[]{:S(2)}, u32[]{:S(2)}) collective-permute-start(f32[12,3712]{1,0:T(8,128)S(1)} %slice_select_fusion), channel_id=1, source_target_pairs={{0,1},{1,0},{2,3},{3,2},{4,5},{5,4},{6,7},{7,6},{8,9},{9,8},{10,11... | collective-permute-start | bytes 534536 | tf_op jit(solution)/shard_map/ppermute | solution.py:13
  182.3 10.7 %collective-permute-start.33 = (bf16[1,12,3584]{2,1,0:T(8,128)(2,1)S(1)}, bf16[1,12,3584]{2,1,0:T(8,128)(2,1)S(1)}, u32[]{:S(2)}, u32[]{:S(2)}) collective-permute-start(bf16[1,12,3584]{2,1,0:T(8,128)(2,1)S(1)} %fusion.40), channel_id=1, source_target_pairs={{64,0},{128,64},{192,128},{256,192},{320,256},{384,320},{448,384},... | collective-permute-start | bytes 258056 | tf_op jit(solution)/shard_map/ppermute | solution.py:139
